TPU v7x, 32 devices: a whole 2x2x4 slice. The times are simulated.
32 devices in a mesh: row: 8 (over y, x, core), col: 4 (over z).
Axes of the slice: x: 2, y: 2, z: 4, core: 2. Of those that a mesh axis runs over, the one named last changes fastest.
Arguments:
- a_blocks: bfloat16 [1024, 16, 128, 128], P(('row', 'col')), may hold values from -0.0625 to 0.0625
- omega: bfloat16 [16384, 256], P('col'), may hold values from -6 to 6
- route_dest: int32 [1024, 1], P(('row', 'col')), may hold values from 0 to 7; in each aligned block of 32 rows (0 to 31, 32 to 63, ...) at most 4 rows name the same one
- row_target: int32 [1024], P(('row', 'col')), may hold values from 0 to 31
- col_target: int32 [1024, 16], P(('row', 'col')), may hold values from 0 to 31
Outputs:
- basis: float32 [32768, 256], P(('row', 'col'))
- factor: float32 [256, 256], replicated
Inputs may be any that keep to these rules, and one draw needn't show every extreme that they name: `route_dest`: among the 32 rows of one device no value appears more than 4 times, and in some device's rows one value appears exactly 4 times.
All inputs are finite; a program needn't handle non-finite values.
Results may differ from a plain program's by a relative error of at most 0.003.
Values may be sent and summed in bfloat16 or wider, within the bound.
A program may use at most 192 MiB of HBM per device.

v0:
```python
import functools

import jax
import jax.numpy as jnp
from jax import lax
from jax.experimental import pallas as pl
from jax.experimental.pallas import tpu as pltpu
from jax.sharding import PartitionSpec as P

RB_DEV = 8
CAP = 4
PANEL = 64
HALVES = 2
WIDE = 4
MESH = pl.DeviceIdType.MESH
VMEM = pl.BlockSpec(memory_space=pltpu.VMEM)
SMEM = pl.BlockSpec(memory_space=pltpu.SMEM)
HIGH = lax.Precision.HIGHEST


def dot_nn(a, b):
    return lax.dot_general(a, b, (((1,), (0,)), ((), ())), precision=HIGH, preferred_element_type=jnp.float32)


def dot_nt(a, b):
    return lax.dot_general(a, b, (((1,), (1,)), ((), ())), precision=HIGH, preferred_element_type=jnp.float32)


def dot_tn(a, b):
    return lax.dot_general(a, b, (((0,), (0,)), ((), ())), precision=HIGH, preferred_element_type=jnp.float32)


def partial_kernel(slot_ref, col_ref, a_ref, omega_ref, out_ref):
    step = pl.program_id(0)
    per_step, groups, order, _ = a_ref.shape
    for local in range(per_step):
        t = step * per_step + local
        total = None
        for g in range(0, groups, 2):
            left = jnp.concatenate([a_ref[local, g], a_ref[local, g + 1]], axis=1)
            c0 = pl.multiple_of(col_ref[t * groups + g] * order, order)
            c1 = pl.multiple_of(col_ref[t * groups + g + 1] * order, order)
            right = jnp.concatenate([omega_ref[pl.ds(c0, order), :], omega_ref[pl.ds(c1, order), :]], axis=0)
            term = jnp.dot(left, right, preferred_element_type=jnp.float32)
            total = term if total is None else total + term
        total = total.astype(jnp.bfloat16)
        half = out_ref.shape[-1]
        for h in range(HALVES):
            out_ref[h, slot_ref[t]] = total[:, h * half:(h + 1) * half]


def partials(slot_of, col_flat, a_blocks, omega, slots):
    targets, groups, order, _ = a_blocks.shape
    width = omega.shape[1]
    per_step = 4
    return pl.pallas_call(
        partial_kernel,
        out_shape=jax.ShapeDtypeStruct((HALVES, slots, order, width // HALVES), jnp.bfloat16),
        grid_spec=pltpu.PrefetchScalarGridSpec(
            num_scalar_prefetch=2,
            grid=(targets // per_step,),
            in_specs=[
                pl.BlockSpec((per_step, groups, order, order), lambda i, *_: (i, 0, 0, 0)),
                pl.BlockSpec(omega.shape, lambda i, *_: (0, 0)),
            ],
            out_specs=pl.BlockSpec((HALVES, slots, order, width // HALVES), lambda i, *_: (0, 0, 0, 0)),
        ),
        compiler_params=pltpu.CompilerParams(vmem_limit_bytes=50 << 20),
    )(slot_of, col_flat, a_blocks, omega)


def row_exchange_kernel(nr, send_ref, srow_ref, got_ref, grow_ref, s_sem, r_sem, s2_sem, r2_sem, own_sem):
    r = lax.axis_index("row")
    c = lax.axis_index("col")
    barrier = pltpu.get_barrier_semaphore()
    for k in range(1, nr):
        pl.semaphore_signal(barrier, inc=1, device_id=(lax.rem(r + k, nr), c), device_id_type=MESH)
    own = pltpu.make_async_copy(send_ref.at[0, r], got_ref.at[r], own_sem.at[0])
    own_rows = pltpu.make_async_copy(srow_ref.at[r], grow_ref.at[r], own_sem.at[1])
    own.start()
    own_rows.start()
    pl.semaphore_wait(barrier, nr - 1)
    copies = []
    for k in range(1, nr):
        d = lax.rem(r + k, nr)
        for src, dst, ss, rs in ((srow_ref, grow_ref, s2_sem, r2_sem), (send_ref.at[0], got_ref, s_sem, r_sem)):
            cp = pltpu.make_async_remote_copy(src.at[d], dst.at[r], ss.at[k], rs.at[k], device_id=(d, c), device_id_type=MESH)
            cp.start()
            copies.append(cp)
    own.wait()
    own_rows.wait()
    for cp in copies:
        cp.wait()


def row_exchange(send, rows, nr):
    dma = pltpu.SemaphoreType.DMA
    return pl.pallas_call(
        functools.partial(row_exchange_kernel, nr),
        out_shape=(jax.ShapeDtypeStruct(send.shape[1:], send.dtype), jax.ShapeDtypeStruct(rows.shape, rows.dtype)),
        in_specs=[VMEM, VMEM],
        out_specs=(VMEM, VMEM),
        scratch_shapes=[dma((nr,)), dma((nr,)), dma((nr,)), dma((nr,)), dma((2,))],
        compiler_params=pltpu.CompilerParams(collective_id=1, has_side_effects=True, vmem_limit_bytes=16 << 20),
    )(send, rows)


def both_exchange_kernel(nr, nc, send_ref, term_ref, got_ref, arrived_ref, s_sem, r_sem, s2_sem, r2_sem, own_sem):
    r = lax.axis_index("row")
    c = lax.axis_index("col")
    own = pltpu.make_async_copy(send_ref.at[1, r], got_ref.at[r], own_sem.at[0])
    own.start()
    greet(nr, nc, r, c)
    copies = []
    for k in range(1, nc):
        d = lax.rem(c + k, nc)
        copies.append(pltpu.make_async_remote_copy(
            term_ref.at[pl.ds(d * RB_DEV, RB_DEV)], arrived_ref.at[k], s2_sem.at[k], r2_sem.at[k],
            device_id=(r, d), device_id_type=MESH))
        copies[-1].start()
    for k in range(1, nr):
        d = lax.rem(r + k, nr)
        copies.append(pltpu.make_async_remote_copy(
            send_ref.at[1, d], got_ref.at[r], s_sem.at[k], r_sem.at[k], device_id=(d, c), device_id_type=MESH))
        copies[-1].start()
    own.wait()
    for cp in copies:
        cp.wait()


def both_exchange(send, term, nr, nc):
    dma = pltpu.SemaphoreType.DMA
    _, order, width = term.shape
    return pl.pallas_call(
        functools.partial(both_exchange_kernel, nr, nc),
        out_shape=(
            jax.ShapeDtypeStruct(send.shape[1:], send.dtype),
            jax.ShapeDtypeStruct((nc, RB_DEV, order, width), term.dtype),
        ),
        in_specs=[VMEM, VMEM],
        out_specs=(VMEM, VMEM),
        scratch_shapes=[dma((nr,)), dma((nr,)), dma((nc,)), dma((nc,)), dma((1,))],
        compiler_params=pltpu.CompilerParams(collective_id=4, has_side_effects=True, vmem_limit_bytes=16 << 20),
    )(send, term)


def gather_sum_kernel(rows_ref, me_ref, got_ref, term_ref, own_ref, acc):
    acc[...] = jnp.zeros_like(acc)

    @pl.loop(0, got_ref.shape[0])
    def _(s):
        row = rows_ref[s]

        @pl.when(row >= 0)
        def _():
            acc[row] = acc[row] + got_ref[s].astype(jnp.float32)

    @pl.loop(0, acc.shape[0])
    def _(b):
        term_ref[b] = acc[b].astype(jnp.bfloat16)

    @pl.loop(0, own_ref.shape[0])
    def _(b):
        own_ref[b] = acc[me_ref[0] * own_ref.shape[0] + b]


def gather_sum(rows, me, got, blocks):
    _, order, width = got.shape
    return pl.pallas_call(
        gather_sum_kernel,
        out_shape=(
            jax.ShapeDtypeStruct((blocks, order, width), jnp.bfloat16),
            jax.ShapeDtypeStruct((RB_DEV, order, width), jnp.float32),
        ),
        in_specs=[SMEM, SMEM, VMEM],
        out_specs=(VMEM, VMEM),
        scratch_shapes=[pltpu.VMEM((blocks, order, width), jnp.float32)],
        compiler_params=pltpu.CompilerParams(vmem_limit_bytes=20 << 20),
    )(rows, me, got)


def greet(nr, nc, r, c):
    barrier = pltpu.get_barrier_semaphore()
    for k in range(1, nr):
        pl.semaphore_signal(barrier, inc=1, device_id=(lax.rem(r + k, nr), c), device_id_type=MESH)
    for k in range(1, nc):
        pl.semaphore_signal(barrier, inc=1, device_id=(r, lax.rem(c + k, nc)), device_id_type=MESH)
    pl.semaphore_wait(barrier, nr - 1 + nc - 1)


def reduce_gram(nr, nc, r, c, gram, landed, cols, full, sems):
    a_s, a_r, b_s, b_r, c_s, c_r = sems
    chunk = gram.shape[0] // nr
    mine = pl.ds(pl.multiple_of(r * chunk, chunk), chunk)
    copies = []
    for k in range(1, nr):
        d = lax.rem(r + k, nr)
        cp = pltpu.make_async_remote_copy(
            gram.at[pl.ds(pl.multiple_of(d * chunk, chunk), chunk), :], landed.at[k], a_s.at[k], a_r.at[k],
            device_id=(d, c), device_id_type=MESH)
        cp.start()
        copies.append(cp)
    total = gram[mine, :]
    for k in range(1, nr):
        copies[k - 1].wait_recv()
        total = total + landed[k]
    cols[c] = total
    across = []
    for k in range(1, nc):
        cp = pltpu.make_async_remote_copy(
            cols.at[c], cols.at[c], b_s.at[k], b_r.at[k], device_id=(r, lax.rem(c + k, nc)), device_id_type=MESH)
        cp.start()
        across.append(cp)
    for cp in across:
        cp.wait_recv()
    total = cols[0]
    for k in range(1, nc):
        total = total + cols[k]
    full[mine, :] = total
    back = []
    for k in range(1, nr):
        cp = pltpu.make_async_remote_copy(
            full.at[mine, :], full.at[mine, :], c_s.at[k], c_r.at[k], device_id=(lax.rem(r + k, nr), c), device_id_type=MESH)
        cp.start()
        back.append(cp)
    for cp in back:
        cp.wait_recv()
    for cp in copies + across + back:
        cp.wait_send()


def gram_scratch(nr, nc, order):
    dma = pltpu.SemaphoreType.DMA
    chunk = order // nr
    return [
        pltpu.VMEM((nr, chunk, order), jnp.float32),
        pltpu.VMEM((nc, chunk, order), jnp.float32),
        pltpu.VMEM((order, order), jnp.float32),
        dma((nr,)), dma((nr,)), dma((nc,)), dma((nc,)), dma((nr,)), dma((nr,)),
    ]


def col_sum_kernel(nr, nc, term_ref, own_ref, arrived0, own0, sketch_ref, out_ref, got, gram, landed, cols, full, *sems):
    r = lax.axis_index("row")
    c = lax.axis_index("col")
    s_sem, r_sem = sems[6], sems[7]
    greet(nr, nc, r, c)
    copies = []
    for k in range(1, nc):
        d = lax.rem(c + k, nc)
        cp = pltpu.make_async_remote_copy(
            term_ref.at[pl.ds(d * RB_DEV, RB_DEV)], got.at[k], s_sem.at[k], r_sem.at[k],
            device_id=(r, d), device_id_type=MESH)
        cp.start()
        copies.append(cp)
    _, order, half = own_ref.shape
    gram[...] = jnp.zeros_like(gram)
    pair = 2 * order

    @pl.loop(0, RB_DEV // 2)
    def _(i):
        pieces = []
        for b in (2 * i, 2 * i + 1):
            total = own0[b]
            for k in range(1, nc):
                total = total + arrived0[k, b].astype(jnp.float32)
            pieces.append(total)
        rows = jnp.concatenate(pieces, axis=0)
        sketch_ref[pl.ds(pl.multiple_of(i * pair, pair), pair), :half] = rows
        gram[:half, :half] += dot_tn(rows, rows)

    for cp in copies:
        cp.wait()

    @pl.loop(0, RB_DEV // 2)
    def _(i):
        pieces = []
        for b in (2 * i, 2 * i + 1):
            total = own_ref[b]
            for k in range(1, nc):
                total = total + got[k, b].astype(jnp.float32)
            pieces.append(total)
        rows = jnp.concatenate(pieces, axis=0)
        part = pl.ds(pl.multiple_of(i * pair, pair), pair)
        sketch_ref[part, half:] = rows
        gram[:, half:] += dot_tn(sketch_ref[part, :], rows)

    gram[half:, :half] = gram[:half, half:].T
    reduce_gram(nr, nc, r, c, gram, landed, cols, full, sems[:6])
    out_ref[...] = full[...]


def col_sum(term, own, arrived0, own0, nr, nc):
    _, order, half = own.shape
    width = HALVES * half
    dma = pltpu.SemaphoreType.DMA
    return pl.pallas_call(
        functools.partial(col_sum_kernel, nr, nc),
        out_shape=(
            jax.ShapeDtypeStruct((RB_DEV * order, width), jnp.float32),
            jax.ShapeDtypeStruct((width, width), jnp.float32),
        ),
        in_specs=[VMEM, VMEM, VMEM, VMEM],
        out_specs=(VMEM, VMEM),
        scratch_shapes=[
            pltpu.VMEM((nc, RB_DEV, order, half), jnp.bfloat16),
            pltpu.VMEM((width, width), jnp.float32),
        ] + gram_scratch(nr, nc, width) + [dma((nc,)), dma((nc,))],
        compiler_params=pltpu.CompilerParams(collective_id=2, has_side_effects=True, vmem_limit_bytes=24 << 20),
    )(term, own, arrived0, own0)


def gram_sum_kernel(nr, nc, gram, out_ref, landed, cols, full, *sems):
    r = lax.axis_index("row")
    c = lax.axis_index("col")
    greet(nr, nc, r, c)
    reduce_gram(nr, nc, r, c, gram, landed, cols, full, sems)
    out_ref[...] = full[...]


def gram_sum(gram, nr, nc):
    return pl.pallas_call(
        functools.partial(gram_sum_kernel, nr, nc),
        out_shape=jax.ShapeDtypeStruct(gram.shape, jnp.float32),
        in_specs=[VMEM],
        out_specs=VMEM,
        scratch_shapes=gram_scratch(nr, nc, gram.shape[0]),
        compiler_params=pltpu.CompilerParams(collective_id=3, has_side_effects=True, vmem_limit_bytes=8 << 20),
    )(gram)


def eliminate(x):
    rows = x.shape[0]
    shape = (8, x.shape[1])
    groups = [x[i:i + 8, :] for i in range(0, rows, 8)]
    sub = lax.broadcasted_iota(jnp.int32, shape, 0)
    for j in range(0, rows, WIDE):
        g, o = divmod(j, 8)
        cols = [[jnp.broadcast_to(groups[i][:, j + l:j + l + 1], shape) for l in range(WIDE)]
                for i in range(g, rows // 8)]
        piv = [[jnp.broadcast_to(cols[0][l][o + k:o + k + 1, :], shape) for l in range(WIDE)] for k in range(WIDE)]
        tops = [jnp.broadcast_to(groups[g][o + k:o + k + 1, :], shape) for k in range(WIDE)]
        recip = []
        for k in range(WIDE):
            recip.append(1.0 / piv[k][k])
            for m in range(k + 1, WIDE):
                q = piv[m][k] * recip[k]
                for l in range(k + 1, WIDE):
                    piv[m][l] = piv[m][l] - q * piv[k][l]
                tops[m] = tops[m] - q * tops[k]
        for i in range(g, rows // 8):
            here = cols[i - g]
            value = groups[i]
            for k in range(WIDE):
                f = here[k] * recip[k]
                for l in range(k + 1, WIDE):
                    here[l] = here[l] - f * piv[k][l]
                value = value - f * tops[k]
            if i == g:
                value = jnp.where(sub >= o + WIDE, value, groups[i])
                for k in range(1, WIDE):
                    value = jnp.where(sub == o + k, tops[k], value)
            groups[i] = value
    return jnp.concatenate(groups, axis=0)


def factor_gram(gram, work, upper, inverse):
    order = gram.shape[0]
    row = lax.broadcasted_iota(jnp.int32, (order, order), 0)
    col = lax.broadcasted_iota(jnp.int32, (order, order), 1)
    work[:, :order] = gram[...]
    work[:, order:] = (row == col).astype(jnp.float32)
    lane = lax.broadcasted_iota(jnp.int32, (PANEL, 2 * PANEL), 1)
    prow = lax.broadcasted_iota(jnp.int32, (PANEL, 2 * PANEL), 0)

    @pl.loop(0, order // PANEL)
    def _(p):
        base = pl.multiple_of(p * PANEL, PANEL)
        tile = work[pl.ds(base, PANEL), pl.ds(pl.multiple_of((p // 2) * 2 * PANEL, 2 * PANEL), 2 * PANEL)]
        tile = jnp.where(p % 2 == 1, pltpu.roll(tile, PANEL, 1), tile)
        x = jnp.where(lane < PANEL, tile, (lane - PANEL == prow).astype(jnp.float32))
        x = eliminate(x)
        diag = jnp.sum(jnp.where(lane == prow, x, 0.0), axis=1, keepdims=True)
        left = pltpu.roll(x, PANEL, 1)[:, :PANEL]
        panel = dot_nn(left, work[pl.ds(base, PANEL), :])
        root = 1.0 / jnp.sqrt(diag)
        pcol = lax.broadcasted_iota(jnp.int32, (PANEL, order), 1)
        pr = lax.broadcasted_iota(jnp.int32, (PANEL, order), 0) + base
        upper[pl.ds(base, PANEL), :] = jnp.where(pcol >= pr, panel[:, :order] * root, 0.0)
        inverse[pl.ds(base, PANEL), :] = jnp.where(pcol <= pr, panel[:, order:] * root, 0.0)

        @pl.when(p < order // PANEL - 1)
        def _():
            half = panel * root
            update = dot_tn(half[:, :order], half)
            below = lax.broadcasted_iota(jnp.int32, (order, 1), 0) >= base + PANEL
            work[...] = jnp.where(below, work[...] - update, work[...])


def first_kernel(gram, sketch, upper, once, second, work, inverse):
    factor_gram(gram, work, upper, inverse)
    second[...] = jnp.zeros_like(second)
    step = 256

    @pl.loop(0, sketch.shape[0] // step)
    def _(i):
        part = pl.ds(pl.multiple_of(i * step, step), step)
        rows = dot_nt(sketch[part, :], inverse[...])
        once[part, :] = rows
        second[...] += dot_tn(rows, rows)


def first_pass(gram, sketch):
    order = gram.shape[0]
    square = jax.ShapeDtypeStruct((order, order), jnp.float32)
    return pl.pallas_call(
        first_kernel,
        out_shape=(square, jax.ShapeDtypeStruct(sketch.shape, jnp.float32), square),
        in_specs=[VMEM, VMEM],
        out_specs=(VMEM, VMEM, VMEM),
        scratch_shapes=[pltpu.VMEM((order, 2 * order), jnp.float32), pltpu.VMEM((order, order), jnp.float32)],
        compiler_params=pltpu.CompilerParams(vmem_limit_bytes=16 << 20),
    )(gram, sketch)


def last_kernel(scale, gram, once, upper_one, basis, factor, work, upper, inverse):
    factor_gram(gram, work, upper, inverse)
    factor[...] = dot_nn(upper[...], upper_one[...]) * (1.0 / scale)
    step = 256

    @pl.loop(0, once.shape[0] // step)
    def _(i):
        part = pl.ds(pl.multiple_of(i * step, step), step)
        basis[part, :] = dot_nt(once[part, :], inverse[...]) * scale


def last_pass(gram, once, upper_one, scale):
    order = gram.shape[0]
    square = pltpu.VMEM((order, order), jnp.float32)
    return pl.pallas_call(
        functools.partial(last_kernel, scale),
        out_shape=(
            jax.ShapeDtypeStruct(once.shape, jnp.float32),
            jax.ShapeDtypeStruct((order, order), jnp.float32),
        ),
        in_specs=[VMEM, VMEM, VMEM],
        out_specs=(VMEM, VMEM),
        scratch_shapes=[pltpu.VMEM((order, 2 * order), jnp.float32), square, square],
        compiler_params=pltpu.CompilerParams(vmem_limit_bytes=16 << 20),
    )(gram, once, upper_one)


def body(nr, nc, a_blocks, omega, route_dest, row_target, col_target):
    targets_here, _, order, _ = a_blocks.shape
    width = omega.shape[1]
    slots = nr * CAP
    destination = route_dest[:, 0]
    positions = jnp.arange(targets_here, dtype=jnp.int32)
    same_owner = destination[:, None] == destination[None, :]
    earlier = positions[None, :] < positions[:, None]
    rank = jnp.sum(jnp.logical_and(same_owner, earlier).astype(jnp.int32), axis=1)
    slot_of = destination * CAP + rank
    slot_ids = jnp.arange(slots, dtype=jnp.int32)
    matches = slot_of[None, :] == slot_ids[:, None]
    send_rows = jnp.sum(jnp.where(matches, row_target[None, :] + 1, 0), axis=1) - 1
    send_rows = jnp.pad(send_rows.reshape(nr, 1, CAP), ((0, 0), (0, 0), (0, 128 - CAP)))
    send_rows = jnp.broadcast_to(send_rows, (nr, 8, 128))
    send = partials(slot_of, col_target.reshape(-1), a_blocks, omega, slots)
    half = width // HALVES
    send = send.reshape(HALVES, nr, CAP, order, half)
    got0, got_rows = row_exchange(send, send_rows, nr)
    me = lax.axis_index("col").astype(jnp.int32).reshape(1)
    rows = got_rows[:, 0, :CAP].reshape(slots)
    term0, own0 = gather_sum(rows, me, got0.reshape(slots, order, half), nc * RB_DEV)
    got1, arrived0 = both_exchange(send, term0, nr, nc)
    term1, own1 = gather_sum(rows, me, got1.reshape(slots, order, half), nc * RB_DEV)
    sketch, gram_one = col_sum(term1, own1, arrived0, own0, nr, nc)
    upper_one, once, gram_part = first_pass(gram_one, sketch)
    gram_two = gram_sum(gram_part, nr, nc)
    scale = float(nr * nc * RB_DEV * order) ** 0.5
    return last_pass(gram_two, once, upper_one, scale)


def solution(mesh):
    nr, nc = mesh.shape["row"], mesh.shape["col"]
    return jax.shard_map(
        functools.partial(body, nr, nc),
        mesh=mesh,
        in_specs=(
            P(("row", "col"), None, None, None),
            P("col", None),
            P(("row", "col"), None),
            P(("row", "col")),
            P(("row", "col"), None),
        ),
        out_specs=(P(("row", "col"), None), P()),
        check_vma=False,
    )
```

profile of v0, /device:TPU:0, one launch (start us, length us, event | category | flops | bytes accessed | tf_op | source)
XLA Modules:
  0.0 156.7 jit_solution(5917032354162362920)
XLA Ops:
  0.6 0.9 convert_reduce_fusion
  1.5 0.7 multiply_add_fusion
  2.2 0.1 select_reduce_fusion
  2.3 0.1 sub.7
  2.4 0.8 copy.8
  3.2 0.1 reshape.43.col_ref
  3.3 11.8 %shard_map.68 = bf16[2,32,128,128]{3,2,1,0:T(8,128)(2,1)S(1)} custom-call(s32[32]{0:T(128)S(1)} %get-tuple-element.28.slot_ref, s32[512]{0:T(512)S(1)} %reshape.43.col_ref, bf16[32,16,128,128]{3,2,1,0:T(8,128)(2,1)} %a_ref.1, bf16[4096,256]{1,0:T(8,128)(2,1)} %omega_ref.1), custom_call_target="tpu_custom_call" | custom-call | tf_op jit(solution)/shard_map/pallas_call | solution.py:56
  15.1 16.4 %shard_map.69 = (bf16[8,4,128,128]{3,2,1,0:T(8,128)(2,1)S(1)}, s32[8,8,128]{2,1,0:T(8,128)S(1)}) custom-call(bf16[2,8,4,128,128]{4,3,2,1,0:T(8,128)(2,1)S(1)} %bitcast.8, s32[8,8,128]{2,1,0:T(8,128)S(1)} %broadcast_in_dim.27.srow_ref), custom_call_target="tpu_custom_call" | custom-call | tf_op jit(solution)/shard_map/pallas_call | solution.py:98
  31.5 0.1 reshape_squeeze.3.rows_ref
  31.6 1.6 shard_map.70
  33.2 24.2 %shard_map.71 = (bf16[8,4,128,128]{3,2,1,0:T(8,128)(2,1)S(1)}, bf16[4,8,128,128]{3,2,1,0:T(8,128)(2,1)S(1)}) custom-call(bf16[2,8,4,128,128]{4,3,2,1,0:T(8,128)(2,1)S(1)} %bitcast.9, bf16[32,128,128]{2,1,0:T(8,128)(2,1)S(1)} %get-tuple-element.17.term_ref), custom_call_target="tpu_custom_call" | custom-call | tf_op jit(solution)/shard_map/pallas_call | solution.py:134
  57.4 1.6 shard_map.72
  59.0 45.3 %shard_map.73 = (f32[1024,256]{1,0:T(8,128)S(1)}, f32[256,256]{1,0:T(8,128)S(1)}) custom-call(bf16[32,128,128]{2,1,0:T(8,128)(2,1)S(1)} %get-tuple-element.19.term_ref, f32[8,128,128]{2,1,0:T(8,128)S(1)} %get-tuple-element.20.own_ref, bf16[4,8,128,128]{3,2,1,0:T(8,128)(2,1)S(1)} %get-tuple-element.21.arrived0, f32[8,128,128]{2,1,0:T(8,128)S(1)} %get-tuple-element.22.own0), custom_call_target="tpu_custom_call" | custom-call | tf_op jit(solution)/shard_map/pallas_call | solution.py:297
  104.3 18.9 %shard_map.74 = (f32[256,256]{1,0:T(8,128)S(1)}, f32[1024,256]{1,0:T(8,128)S(1)}, f32[256,256]{1,0:T(8,128)S(1)}) custom-call(f32[256,256]{1,0:T(8,128)S(1)} %get-tuple-element.23.gram, f32[1024,256]{1,0:T(8,128)S(1)} %get-tuple-element.24.sketch), custom_call_target="tpu_custom_call" | custom-call | tf_op jit(solution)/shard_map/pallas_call | solution.py:416
  123.2 16.2 %shard_map.75.gram = f32[256,256]{1,0:T(8,128)S(1)} custom-call(f32[256,256]{1,0:T(8,128)S(1)} %get-tuple-element.25.gram), custom_call_target="tpu_custom_call" | custom-call | tf_op jit(solution)/shard_map/pallas_call | solution.py:322
  139.4 17.3 %shard_map.76 = (f32[1024,256]{1,0:T(8,128)}, f32[256,256]{1,0:T(8,128)}) custom-call(f32[256,256]{1,0:T(8,128)S(1)} %shard_map.75.gram, f32[1024,256]{1,0:T(8,128)S(1)} %get-tuple-element.26.once, f32[256,256]{1,0:T(8,128)S(1)} %get-tuple-element.27.upper_one), custom_call_target="tpu_custom_call" | custom-call | tf_op jit(solution)/shard_map/pallas_call | solution.py:440
  (4 shorter events, 0.0 us)
where the time goes:
time: 157 us
  Pallas kernels  153 us (97%)
  other arithmetic  1.71 us (1%)
    pallas_call x1, Pallas kernels, col_sum(): pl.pallas_call(functools.partial(col_sum_kernel, nr, nc), out_shape=(jax....  45.3 us
    pallas_call x1, Pallas kernels, both_exchange(): pl.pallas_call(functools.partial(both_exchange_kernel, nr, nc), out_shape...  24.2 us
    pallas_call x1, Pallas kernels, first_pass(): pl.pallas_call(first_kernel, out_shape=(square, jax.ShapeDtypeStruct(sket...  18.9 us
    pallas_call x1, Pallas kernels, last_pass(): pl.pallas_call(functools.partial(last_kernel, scale), out_shape=(jax.Shap...  17.3 us
    pallas_call x1, Pallas kernels, row_exchange(): pl.pallas_call(functools.partial(row_exchange_kernel, nr), out_shape=(jax...  16.4 us
    pallas_call x1, Pallas kernels, gram_sum(): pl.pallas_call(functools.partial(gram_sum_kernel, nr, nc), out_shape=jax....  16.2 us
    pallas_call x1, Pallas kernels, partials(): pl.pallas_call(partial_kernel, out_shape=jax.ShapeDtypeStruct((HALVES, sl...  11.8 us

commit v1 on v0

v1 whole, which is shorter than its diff:
```python
import functools

import jax
import jax.numpy as jnp
from jax import lax
from jax.experimental import pallas as pl
from jax.experimental.pallas import tpu as pltpu
from jax.sharding import PartitionSpec as P

RB_DEV = 8
CAP = 4
PANEL = 64
LOADS = 4
NOWHERE = 1 << 20
CHUNKS = 4
WIDE = 4
MESH = pl.DeviceIdType.MESH
VMEM = pl.BlockSpec(memory_space=pltpu.VMEM)
SMEM = pl.BlockSpec(memory_space=pltpu.SMEM)
HIGH = lax.Precision.HIGHEST


def dot_nn(a, b):
    return lax.dot_general(a, b, (((1,), (0,)), ((), ())), precision=HIGH, preferred_element_type=jnp.float32)


def dot_nt(a, b):
    return lax.dot_general(a, b, (((1,), (1,)), ((), ())), precision=HIGH, preferred_element_type=jnp.float32)


def dot_tn(a, b):
    return lax.dot_general(a, b, (((0,), (0,)), ((), ())), precision=HIGH, preferred_element_type=jnp.float32)


def partial_kernel(dest_ref, target_ref, col_ref, a_hbm, omega_hbm, out_ref, row_ref, a_buf, omega_buf, slot_of, count, a_sem, omega_sem):
    targets, groups, order, _ = a_buf.shape
    chunks, slots, rq, _ = out_ref.shape
    loads = targets // LOADS

    def fetch(i):
        part = pl.ds(i * LOADS, LOADS)
        return pltpu.make_async_copy(a_hbm.at[part], a_buf.at[part], a_sem.at[i])

    load_omega = pltpu.make_async_copy(omega_hbm, omega_buf, omega_sem.at[0])
    load_omega.start()
    for i in range(loads):
        fetch(i).start()
    owners = slots // CAP
    row_ref[...] = jnp.full(row_ref.shape, NOWHERE, jnp.int32)
    if slots > targets:
        out_ref[...] = jnp.zeros(out_ref.shape, out_ref.dtype)
    for d in range(owners):
        count[d] = 0

    @pl.loop(0, targets)
    def _(t):
        d = dest_ref[t]
        rank = count[d]
        count[d] = rank + 1
        slot_of[t] = d * CAP + rank
        row_ref[d, pl.ds(rank, 1), :] = jnp.full((1, row_ref.shape[2]), target_ref[t], jnp.int32)

    load_omega.wait()

    @pl.loop(0, loads)
    def _(i):
        fetch(i).wait()
        for local in range(LOADS):
            t = i * LOADS + local
            total = None
            for g in range(0, groups, 2):
                left = jnp.concatenate([a_buf[t, g], a_buf[t, g + 1]], axis=1)
                c0 = pl.multiple_of(col_ref[t * groups + g] * order, order)
                c1 = pl.multiple_of(col_ref[t * groups + g + 1] * order, order)
                right = jnp.concatenate([omega_buf[pl.ds(c0, order), :], omega_buf[pl.ds(c1, order), :]], axis=0)
                term = jnp.dot(left, right, preferred_element_type=jnp.float32)
                total = term if total is None else total + term
            total = total.astype(jnp.bfloat16)
            for q in range(chunks):
                out_ref[q, slot_of[t]] = total[q * rq:(q + 1) * rq]


def partials(destination, row_target, col_flat, a_blocks, omega, slots):
    targets, _, order, _ = a_blocks.shape
    width = omega.shape[1]
    dma = pltpu.SemaphoreType.DMA
    any_space = pl.BlockSpec(memory_space=pl.ANY)
    return pl.pallas_call(
        partial_kernel,
        out_shape=(
            jax.ShapeDtypeStruct((CHUNKS, slots, order // CHUNKS, width), jnp.bfloat16),
            jax.ShapeDtypeStruct((slots // CAP, 8, 128), jnp.int32),
        ),
        in_specs=[SMEM, SMEM, SMEM, any_space, any_space],
        out_specs=(VMEM, VMEM),
        scratch_shapes=[
            pltpu.VMEM(a_blocks.shape, a_blocks.dtype),
            pltpu.VMEM(omega.shape, omega.dtype),
            pltpu.SMEM((targets,), jnp.int32),
            pltpu.SMEM((slots // CAP,), jnp.int32),
            dma((targets // LOADS,)), dma((1,)),
        ],
        compiler_params=pltpu.CompilerParams(vmem_limit_bytes=40 << 20),
    )(destination, row_target, col_flat, a_blocks, omega)


def greet(nr, nc, r, c):
    barrier = pltpu.get_barrier_semaphore()
    for k in range(1, nr):
        pl.semaphore_signal(barrier, inc=1, device_id=(lax.rem(r + k, nr), c), device_id_type=MESH)
    for k in range(1, nc):
        pl.semaphore_signal(barrier, inc=1, device_id=(r, lax.rem(c + k, nc)), device_id_type=MESH)
    pl.semaphore_wait(barrier, nr - 1 + nc - 1)


def reduce_packed(nr, nc, r, c, gram, landed, cols, full, sems):
    a_s, a_r, b_s, b_r, c_s, c_r = sems
    chunk = gram.shape[0] // nr
    mine = pl.ds(pl.multiple_of(r * chunk, chunk), chunk)
    copies = []
    for k in range(1, nr):
        d = lax.rem(r + k, nr)
        cp = pltpu.make_async_remote_copy(
            gram.at[pl.ds(pl.multiple_of(d * chunk, chunk), chunk), :], landed.at[k], a_s.at[k], a_r.at[k],
            device_id=(d, c), device_id_type=MESH)
        cp.start()
        copies.append(cp)
    total = gram[mine, :]
    for k in range(1, nr):
        copies[k - 1].wait_recv()
        total = total + landed[k]
    cols[c] = total
    across = []
    for k in range(1, nc):
        cp = pltpu.make_async_remote_copy(
            cols.at[c], cols.at[c], b_s.at[k], b_r.at[k], device_id=(r, lax.rem(c + k, nc)), device_id_type=MESH)
        cp.start()
        across.append(cp)
    for cp in across:
        cp.wait_recv()
    total = cols[0]
    for k in range(1, nc):
        total = total + cols[k]
    full[mine, :] = total
    back = []
    for k in range(1, nr):
        cp = pltpu.make_async_remote_copy(
            full.at[mine, :], full.at[mine, :], c_s.at[k], c_r.at[k], device_id=(lax.rem(r + k, nr), c), device_id_type=MESH)
        cp.start()
        back.append(cp)
    for cp in back:
        cp.wait_recv()
    for cp in copies + across + back:
        cp.wait_send()


def packed_scratch(nr, nc, width):
    dma = pltpu.SemaphoreType.DMA
    half = width // 2
    chunk = 3 * half // nr
    return [
        pltpu.VMEM((3 * half, half), jnp.float32),
        pltpu.VMEM((nr, chunk, half), jnp.float32),
        pltpu.VMEM((nc, chunk, half), jnp.float32),
        pltpu.VMEM((3 * half, half), jnp.float32),
        dma((nr,)), dma((nr,)), dma((nc,)), dma((nc,)), dma((nr,)), dma((nr,)),
    ]


def sum_gram(nr, nc, r, c, gram, out_ref, packed, landed, cols, full, sems):
    half = gram.shape[0] // 2
    packed[:half, :] = gram[:half, :half]
    packed[half:2 * half, :] = gram[:half, half:]
    packed[2 * half:, :] = gram[half:, half:]
    reduce_packed(nr, nc, r, c, packed, landed, cols, full, sems)
    out_ref[:half, :half] = full[:half, :]
    side = full[half:2 * half, :]
    out_ref[:half, half:] = side
    out_ref[half:, :half] = side.T
    out_ref[half:, half:] = full[2 * half:, :]


def arrange(rows, slots):
    count = rows.shape[0]
    i = lax.broadcasted_iota(jnp.int32, rows.shape, 0)
    j = lax.broadcasted_iota(jnp.int32, rows.shape, 1)
    across = jnp.sum(jnp.where(i == j, rows, 0), axis=0, keepdims=True)
    ahead = jnp.logical_or(across < rows, jnp.logical_and(across == rows, j < i))
    ahead = jnp.logical_and(ahead, j < count)
    rank = jnp.sum(ahead.astype(jnp.int32), axis=1, keepdims=True)
    slot = (i // 8) * CAP + lax.rem(i, 8)
    order = jnp.sum(jnp.where(rank == j, slot, 0), axis=0, keepdims=True)
    here = jnp.sum(jnp.where(rank == j, rows, 0), axis=0, keepdims=True)
    before = jnp.sum(jnp.where(rank == j - 1, rows, 0), axis=0, keepdims=True)
    keep = jnp.logical_and(here == before, j[:1] > 0).astype(jnp.int32)
    last = jnp.max(jnp.where(rows == j, rank, -1), axis=0, keepdims=True)
    valid = (last >= 0).astype(jnp.int32)
    order = jnp.minimum(order, slots - 1)
    last = jnp.clip(last, 0, slots - 1)
    return jnp.concatenate([order, keep, last, valid], axis=0)


def sketch_kernel(nr, nc, send_ref, row_ref, sketch_ref, out_ref, *refs):
    chunks, _, _, rq, width = send_ref.shape
    gots, refs = refs[:chunks], refs[chunks:]
    (rows_in, meta, table, prefix, term, to_right, to_left, total, gram, row_s, row_r, own_s,
     send_s, send_r, right_s, right_r, left_s, left_r), refs = refs[:18], refs[18:]
    slots = nr * CAP
    blocks = nc * RB_DEV
    r = lax.axis_index("row")
    c = lax.axis_index("col")

    def route(k):
        d = lax.rem(r + k, nr)
        return pltpu.make_async_remote_copy(
            row_ref.at[d], rows_in.at[r], row_s.at[k], row_r.at[k], device_id=(d, c), device_id_type=MESH)

    def swap(q, k):
        d = lax.rem(r + k, nr)
        return pltpu.make_async_remote_copy(
            send_ref.at[q, d], gots[q].at[pl.ds(r * CAP, CAP)], send_s.at[q, k], send_r.at[q, k],
            device_id=(d, c), device_id_type=MESH)

    def keep_own(q):
        return pltpu.make_async_copy(send_ref.at[q, r], gots[q].at[pl.ds(r * CAP, CAP)], own_s.at[q])

    def hop_right(q, d):
        return pltpu.make_async_remote_copy(
            to_right.at[q, d], to_right.at[q, d], right_s.at[q, d], right_r.at[q, d],
            device_id=(r, lax.rem(c + 1, nc)), device_id_type=MESH)

    def hop_left(q, d):
        return pltpu.make_async_remote_copy(
            to_left.at[q, d], to_left.at[q, d], left_s.at[q, d], left_r.at[q, d],
            device_id=(r, lax.rem(c + nc - 1, nc)), device_id_type=MESH)

    for q in range(chunks):
        keep_own(q).start()
    own_rows = pltpu.make_async_copy(row_ref.at[r], rows_in.at[r], own_s.at[chunks])
    own_rows.start()
    greet(nr, nc, r, c)
    for k in range(1, nr):
        route(k).start()
    for k in range(1, nr):
        swap(0, k).start()
    gram[...] = jnp.zeros_like(gram)
    own_rows.wait()
    for k in range(1, nr):
        route(k).wait_recv()
    meta[...] = jnp.zeros_like(meta)
    meta[:4, :] = arrange(rows_in[...].reshape(nr * 8, 128), slots)
    to_table = pltpu.make_async_copy(meta, table, own_s.at[chunks + 1])
    to_table.start()
    to_table.wait()

    def collect(q):
        keep_own(q).wait()
        for k in range(1, nr):
            swap(q, k).wait_recv()
        if q + 1 < chunks:
            for k in range(1, nr):
                swap(q + 1, k).start()
        got = gots[q]

        def add(k, acc):
            acc = acc * table[1, k].astype(jnp.float32) + got[table[0, k]].astype(jnp.float32)
            prefix[k] = acc
            return acc

        lax.fori_loop(0, slots, add, jnp.zeros((rq, width), jnp.float32), unroll=4)

        @pl.loop(0, blocks, unroll=4)
        def _(b):
            term[q % 2, b] = prefix[table[2, b]] * table[3, b].astype(jnp.float32)

        @pl.when(c == 0)
        def _():
            for d in range(nc - 1, 0, -1):
                to_right[q, d] = term[q % 2, d * RB_DEV:(d + 1) * RB_DEV].astype(jnp.bfloat16)
                hop_right(q, d).start()

        @pl.when(c == nc - 1)
        def _():
            for d in range(nc - 1):
                to_left[q, d] = term[q % 2, d * RB_DEV:(d + 1) * RB_DEV].astype(jnp.bfloat16)
                hop_left(q, d).start()

    def pass_on(q):
        for k in range(nc - 1, 0, -1):
            @pl.when(jnp.logical_and(c > 0, c + k < nc))
            def _():
                d = c + k
                hop_right(q, d).wait_recv()
                mine = term[q % 2, pl.ds(d * RB_DEV, RB_DEV)]
                to_right[q, d] = (to_right[q, d].astype(jnp.float32) + mine).astype(jnp.bfloat16)
                hop_right(q, d).start()

            @pl.when(jnp.logical_and(c < nc - 1, c - k >= 0))
            def _():
                d = c - k
                hop_left(q, d).wait_recv()
                mine = term[q % 2, pl.ds(d * RB_DEV, RB_DEV)]
                to_left[q, d] = (to_left[q, d].astype(jnp.float32) + mine).astype(jnp.bfloat16)
                hop_left(q, d).start()

        total[...] = term[q % 2, pl.ds(c * RB_DEV, RB_DEV)]

        @pl.when(c > 0)
        def _():
            hop_right(q, c).wait_recv()
            total[...] += to_right[q, c].astype(jnp.float32)

        @pl.when(c < nc - 1)
        def _():
            hop_left(q, c).wait_recv()
            total[...] += to_left[q, c].astype(jnp.float32)

        for b in range(RB_DEV):
            start = b * chunks * rq + q * rq
            sketch_ref[start:start + rq, :] = total[b]
        rows = total[...].reshape(RB_DEV * rq, width)
        gram[...] += dot_tn(rows, rows)

    for q in range(chunks):
        collect(q)
        if q > 0:
            pass_on(q - 1)
    pass_on(chunks - 1)
    sum_gram(nr, nc, r, c, gram, out_ref, *refs[:4], refs[4:])
    for k in range(1, nr):
        route(k).wait_send()
    for q in range(chunks):
        for k in range(1, nr):
            swap(q, k).wait_send()
        for k in range(1, nc):
            @pl.when(c + k < nc)
            def _():
                hop_right(q, c + k).wait_send()

            @pl.when(c - k >= 0)
            def _():
                hop_left(q, c - k).wait_send()


def make_sketch(send, rows, nr, nc):
    chunks, _, _, rq, width = send.shape
    dma = pltpu.SemaphoreType.DMA
    slots, blocks = nr * CAP, nc * RB_DEV
    hops = pltpu.VMEM((chunks, nc, RB_DEV, rq, width), jnp.bfloat16)
    return pl.pallas_call(
        functools.partial(sketch_kernel, nr, nc),
        out_shape=(
            jax.ShapeDtypeStruct((RB_DEV * chunks * rq, width), jnp.float32),
            jax.ShapeDtypeStruct((width, width), jnp.float32),
        ),
        in_specs=[VMEM, VMEM],
        out_specs=(VMEM, VMEM),
        scratch_shapes=[pltpu.VMEM((slots, rq, width), jnp.bfloat16)] * chunks + [
            pltpu.VMEM((nr, 8, 128), jnp.int32),
            pltpu.VMEM((8, 128), jnp.int32),
            pltpu.SMEM((8, 128), jnp.int32),
            pltpu.VMEM((slots, rq, width), jnp.float32),
            pltpu.VMEM((2, blocks, rq, width), jnp.float32),
            hops, hops,
            pltpu.VMEM((RB_DEV, rq, width), jnp.float32),
            pltpu.VMEM((width, width), jnp.float32),
            dma((nr,)), dma((nr,)), dma((chunks + 2,)),
            dma((chunks, nr)), dma((chunks, nr)),
            dma((chunks, nc)), dma((chunks, nc)), dma((chunks, nc)), dma((chunks, nc)),
        ] + packed_scratch(nr, nc, width),
        compiler_params=pltpu.CompilerParams(collective_id=1, has_side_effects=True, vmem_limit_bytes=32 << 20),
    )(send, rows)


def gram_sum_kernel(nr, nc, gram, out_ref, packed, landed, cols, full, *sems):
    r = lax.axis_index("row")
    c = lax.axis_index("col")
    greet(nr, nc, r, c)
    sum_gram(nr, nc, r, c, gram, out_ref, packed, landed, cols, full, sems)


def gram_sum(gram, nr, nc):
    return pl.pallas_call(
        functools.partial(gram_sum_kernel, nr, nc),
        out_shape=jax.ShapeDtypeStruct(gram.shape, jnp.float32),
        in_specs=[VMEM],
        out_specs=VMEM,
        scratch_shapes=packed_scratch(nr, nc, gram.shape[0]),
        compiler_params=pltpu.CompilerParams(collective_id=3, has_side_effects=True, vmem_limit_bytes=8 << 20),
    )(gram)


def eliminate(x):
    rows = x.shape[0]
    shape = (8, x.shape[1])
    groups = [x[i:i + 8, :] for i in range(0, rows, 8)]
    sub = lax.broadcasted_iota(jnp.int32, shape, 0)
    for j in range(0, rows, WIDE):
        g, o = divmod(j, 8)
        cols = [[jnp.broadcast_to(groups[i][:, j + l:j + l + 1], shape) for l in range(WIDE)]
                for i in range(g, rows // 8)]
        piv = [[jnp.broadcast_to(cols[0][l][o + k:o + k + 1, :], shape) for l in range(WIDE)] for k in range(WIDE)]
        tops = [jnp.broadcast_to(groups[g][o + k:o + k + 1, :], shape) for k in range(WIDE)]
        recip = []
        for k in range(WIDE):
            recip.append(1.0 / piv[k][k])
            for m in range(k + 1, WIDE):
                q = piv[m][k] * recip[k]
                for l in range(k + 1, WIDE):
                    piv[m][l] = piv[m][l] - q * piv[k][l]
                tops[m] = tops[m] - q * tops[k]
        for i in range(g, rows // 8):
            here = cols[i - g]
            value = groups[i]
            for k in range(WIDE):
                f = here[k] * recip[k]
                for l in range(k + 1, WIDE):
                    here[l] = here[l] - f * piv[k][l]
                value = value - f * tops[k]
            if i == g:
                value = jnp.where(sub >= o + WIDE, value, groups[i])
                for k in range(1, WIDE):
                    value = jnp.where(sub == o + k, tops[k], value)
            groups[i] = value
    return jnp.concatenate(groups, axis=0)


def factor_gram(gram, work, upper, inverse):
    order = gram.shape[0]
    row = lax.broadcasted_iota(jnp.int32, (order, order), 0)
    col = lax.broadcasted_iota(jnp.int32, (order, order), 1)
    work[:, :order] = gram[...]
    work[:, order:] = (row == col).astype(jnp.float32)
    lane = lax.broadcasted_iota(jnp.int32, (PANEL, 2 * PANEL), 1)
    prow = lax.broadcasted_iota(jnp.int32, (PANEL, 2 * PANEL), 0)

    @pl.loop(0, order // PANEL)
    def _(p):
        base = pl.multiple_of(p * PANEL, PANEL)
        tile = work[pl.ds(base, PANEL), pl.ds(pl.multiple_of((p // 2) * 2 * PANEL, 2 * PANEL), 2 * PANEL)]
        tile = jnp.where(p % 2 == 1, pltpu.roll(tile, PANEL, 1), tile)
        x = jnp.where(lane < PANEL, tile, (lane - PANEL == prow).astype(jnp.float32))
        x = eliminate(x)
        diag = jnp.sum(jnp.where(lane == prow, x, 0.0), axis=1, keepdims=True)
        left = pltpu.roll(x, PANEL, 1)[:, :PANEL]
        panel = dot_nn(left, work[pl.ds(base, PANEL), :])
        root = 1.0 / jnp.sqrt(diag)
        pcol = lax.broadcasted_iota(jnp.int32, (PANEL, order), 1)
        pr = lax.broadcasted_iota(jnp.int32, (PANEL, order), 0) + base
        upper[pl.ds(base, PANEL), :] = jnp.where(pcol >= pr, panel[:, :order] * root, 0.0)
        inverse[pl.ds(base, PANEL), :] = jnp.where(pcol <= pr, panel[:, order:] * root, 0.0)

        @pl.when(p < order // PANEL - 1)
        def _():
            half = panel * root
            update = dot_tn(half[:, :order], half)
            below = lax.broadcasted_iota(jnp.int32, (order, 1), 0) >= base + PANEL
            work[...] = jnp.where(below, work[...] - update, work[...])


def first_kernel(gram, sketch, upper, once, second, work, inverse):
    factor_gram(gram, work, upper, inverse)
    second[...] = jnp.zeros_like(second)
    step = 256

    @pl.loop(0, sketch.shape[0] // step)
    def _(i):
        part = pl.ds(pl.multiple_of(i * step, step), step)
        rows = dot_nt(sketch[part, :], inverse[...])
        once[part, :] = rows
        second[...] += dot_tn(rows, rows)


def first_pass(gram, sketch):
    order = gram.shape[0]
    square = jax.ShapeDtypeStruct((order, order), jnp.float32)
    return pl.pallas_call(
        first_kernel,
        out_shape=(square, jax.ShapeDtypeStruct(sketch.shape, jnp.float32), square),
        in_specs=[VMEM, VMEM],
        out_specs=(VMEM, VMEM, VMEM),
        scratch_shapes=[pltpu.VMEM((order, 2 * order), jnp.float32), pltpu.VMEM((order, order), jnp.float32)],
        compiler_params=pltpu.CompilerParams(vmem_limit_bytes=16 << 20),
    )(gram, sketch)


def last_kernel(scale, gram, once, upper_one, basis, factor, work, upper, inverse):
    factor_gram(gram, work, upper, inverse)
    factor[...] = dot_nn(upper[...], upper_one[...]) * (1.0 / scale)
    step = 256

    @pl.loop(0, once.shape[0] // step)
    def _(i):
        part = pl.ds(pl.multiple_of(i * step, step), step)
        basis[part, :] = dot_nt(once[part, :], inverse[...]) * scale


def last_pass(gram, once, upper_one, scale):
    order = gram.shape[0]
    square = pltpu.VMEM((order, order), jnp.float32)
    return pl.pallas_call(
        functools.partial(last_kernel, scale),
        out_shape=(
            jax.ShapeDtypeStruct(once.shape, jnp.float32),
            jax.ShapeDtypeStruct((order, order), jnp.float32),
        ),
        in_specs=[VMEM, VMEM, VMEM],
        out_specs=(VMEM, VMEM),
        scratch_shapes=[pltpu.VMEM((order, 2 * order), jnp.float32), square, square],
        compiler_params=pltpu.CompilerParams(vmem_limit_bytes=16 << 20),
    )(gram, once, upper_one)


def body(nr, nc, a_blocks, omega, route_dest, row_target, col_target):
    order = a_blocks.shape[2]
    width = omega.shape[1]
    slots = nr * CAP
    send, rows = partials(route_dest.reshape(-1), row_target, col_target.reshape(-1), a_blocks, omega, slots)
    send = send.reshape(CHUNKS, nr, CAP, order // CHUNKS, width)
    sketch, gram_one = make_sketch(send, rows, nr, nc)
    upper_one, once, gram_part = first_pass(gram_one, sketch)
    gram_two = gram_sum(gram_part, nr, nc)
    scale = float(nr * nc * RB_DEV * order) ** 0.5
    return last_pass(gram_two, once, upper_one, scale)


def solution(mesh):
    nr, nc = mesh.shape["row"], mesh.shape["col"]
    return jax.shard_map(
        functools.partial(body, nr, nc),
        mesh=mesh,
        in_specs=(
            P(("row", "col"), None, None, None),
            P("col", None),
            P(("row", "col"), None),
            P(("row", "col")),
            P(("row", "col"), None),
        ),
        out_specs=(P(("row", "col"), None), P()),
        check_vma=False,
    )
```

time: 157 us -> 137 us (0.87)
  Pallas kernels: 153 us -> 132 us
  local copies, waits for them, and re-layouts: 1.05 us -> 3.76 us
  other arithmetic: 1.71 us -> 0 us
    pallas_call x6 -> x2, Pallas kernels: 101 us -> 82.1 us  [the longest x1 73.8 us: make_sketch(): pl.pallas_call(functools.partial(sketch_kernel, nr, nc), out_shape=(jax.S...]
    unnamed x1 -> x7, local copies, waits for them, and re-layouts: 0.78 us -> 3.68 us
    pallas_call x1, Pallas kernels: 16.2 us -> 13.9 us  [gram_sum(): pl.pallas_call(functools.partial(gram_sum_kernel, nr, nc), out_shape=jax....]
where the time goes in v1:
time: 137 us
  Pallas kernels  132 us (96%)
  local copies, waits for them, and re-layouts  3.76 us (3%)
    pallas_call x1, Pallas kernels, make_sketch(): pl.pallas_call(functools.partial(sketch_kernel, nr, nc), out_shape=(jax.S...  73.8 us
    pallas_call x1, Pallas kernels, first_pass(): pl.pallas_call(first_kernel, out_shape=(square, jax.ShapeDtypeStruct(sket...  18.9 us
    pallas_call x1, Pallas kernels, last_pass(): pl.pallas_call(functools.partial(last_kernel, scale), out_shape=(jax.Shap...  17.3 us
    pallas_call x1, Pallas kernels, gram_sum(): pl.pallas_call(functools.partial(gram_sum_kernel, nr, nc), out_shape=jax....  13.9 us
    pallas_call x1, Pallas kernels, partials(): pl.pallas_call(partial_kernel, out_shape=(jax.ShapeDtypeStruct((CHUNKS, s...  8.31 us
    unnamed x7, local copies, waits for them, and re-layouts  3.68 us

profile of v1, /device:TPU:0, one launch (start us, length us, event | category | flops | bytes accessed | tf_op | source)
XLA Modules:
  0.0 136.6 jit_solution(5908868717464367326)
XLA Ops:
  0.6 0.8 copy.7
  1.4 0.1 reshape.14.col_ref
  1.5 0.0 copy-start
  1.5 1.6 %copy-done = bf16[4096,256]{1,0:T(8,128)(2,1)S(1)} copy-done((bf16[4096,256]{1,0:T(8,128)(2,1)S(1)}, bf16[4096,256]{1,0:T(8,128)(2,1)}, u32[]{:S(2)}) %copy-start) | copy-done | bytes 2097176
  3.1 0.0 copy-start.1
  3.1 0.7 copy-done.1
  3.7 0.0 copy-start.2
  3.7 0.7 copy-done.2
  4.4 8.3 %shard_map.68 = (bf16[4,32,32,256]{3,2,1,0:T(8,128)(2,1)S(1)}, s32[8,8,128]{2,1,0:T(8,128)S(1)}) custom-call(s32[32]{0:T(128)S(1)} %bitcast.3, s32[32]{0:T(128)S(1)} %copy-done.2, s32[512]{0:T(512)S(1)} %reshape.14.col_ref, bf16[32,16,128,128]{3,2,1,0:T(8,128)(2,1)} %a_hbm.1, bf16[4096,256]{1,0:T(8,128)(2,1)S(1)} %copy-done), custom_call_target="tpu_custom_call" | custom-call | tf_op jit(solution)/shard_map/pallas_call | solution.py:88
  12.7 73.8 %shard_map.69 = (f32[1024,256]{1,0:T(8,128)S(1)}, f32[256,256]{1,0:T(8,128)S(1)}) custom-call(bf16[4,8,4,32,256]{4,3,2,1,0:T(8,128)(2,1)S(1)} %bitcast.2, s32[8,8,128]{2,1,0:T(8,128)S(1)} %get-tuple-element.10.row_ref), custom_call_target="tpu_custom_call" | custom-call | tf_op jit(solution)/shard_map/pallas_call | solution.py:350
  86.5 18.9 %shard_map.70 = (f32[256,256]{1,0:T(8,128)S(1)}, f32[1024,256]{1,0:T(8,128)S(1)}, f32[256,256]{1,0:T(8,128)S(1)}) custom-call(f32[256,256]{1,0:T(8,128)S(1)} %get-tuple-element.11.gram, f32[1024,256]{1,0:T(8,128)S(1)} %get-tuple-element.12.sketch), custom_call_target="tpu_custom_call" | custom-call | tf_op jit(solution)/shard_map/pallas_call | solution.py:477
  105.4 13.9 %shard_map.71.gram = f32[256,256]{1,0:T(8,128)S(1)} custom-call(f32[256,256]{1,0:T(8,128)S(1)} %get-tuple-element.13.gram), custom_call_target="tpu_custom_call" | custom-call | tf_op jit(solution)/shard_map/pallas_call | solution.py:383
  119.3 17.3 %shard_map.72 = (f32[1024,256]{1,0:T(8,128)}, f32[256,256]{1,0:T(8,128)}) custom-call(f32[256,256]{1,0:T(8,128)S(1)} %shard_map.71.gram, f32[1024,256]{1,0:T(8,128)S(1)} %get-tuple-element.14.once, f32[256,256]{1,0:T(8,128)S(1)} %get-tuple-element.15.upper_one), custom_call_target="tpu_custom_call" | custom-call | tf_op jit(solution)/shard_map/pallas_call | solution.py:501
Async XLA Ops:
  1.5 1.6 %copy-start = (bf16[4096,256]{1,0:T(8,128)(2,1)S(1)}, bf16[4096,256]{1,0:T(8,128)(2,1)}, u32[]{:S(2)}) copy-start(bf16[4096,256]{1,0:T(8,128)(2,1)} %omega_hbm.1) | copy-start | bytes 6291460
  3.1 0.7 copy-start.1
  3.7 0.7 copy-start.2

commit v2 on v1

--- a/solution.py
+++ b/solution.py
@@ -12,7 +12,9 @@
 PANEL = 64
 LOADS = 4
 NOWHERE = 1 << 20
-CHUNKS = 4
+INFLATION = 2.0
+CHUNKS = 8
+WINDOW = 2
 WIDE = 4
 MESH = pl.DeviceIdType.MESH
 VMEM = pl.BlockSpec(memory_space=pltpu.VMEM)
@@ -32,85 +34,38 @@
     return lax.dot_general(a, b, (((0,), (0,)), ((), ())), precision=HIGH, preferred_element_type=jnp.float32)
 
 
-def partial_kernel(dest_ref, target_ref, col_ref, a_hbm, omega_hbm, out_ref, row_ref, a_buf, omega_buf, slot_of, count, a_sem, omega_sem):
-    targets, groups, order, _ = a_buf.shape
-    chunks, slots, rq, _ = out_ref.shape
-    loads = targets // LOADS
-
-    def fetch(i):
-        part = pl.ds(i * LOADS, LOADS)
-        return pltpu.make_async_copy(a_hbm.at[part], a_buf.at[part], a_sem.at[i])
-
-    load_omega = pltpu.make_async_copy(omega_hbm, omega_buf, omega_sem.at[0])
-    load_omega.start()
-    for i in range(loads):
-        fetch(i).start()
-    owners = slots // CAP
-    row_ref[...] = jnp.full(row_ref.shape, NOWHERE, jnp.int32)
-    if slots > targets:
-        out_ref[...] = jnp.zeros(out_ref.shape, out_ref.dtype)
-    for d in range(owners):
-        count[d] = 0
-
-    @pl.loop(0, targets)
-    def _(t):
-        d = dest_ref[t]
-        rank = count[d]
-        count[d] = rank + 1
-        slot_of[t] = d * CAP + rank
-        row_ref[d, pl.ds(rank, 1), :] = jnp.full((1, row_ref.shape[2]), target_ref[t], jnp.int32)
-
-    load_omega.wait()
-
-    @pl.loop(0, loads)
-    def _(i):
-        fetch(i).wait()
-        for local in range(LOADS):
-            t = i * LOADS + local
-            total = None
-            for g in range(0, groups, 2):
-                left = jnp.concatenate([a_buf[t, g], a_buf[t, g + 1]], axis=1)
-                c0 = pl.multiple_of(col_ref[t * groups + g] * order, order)
-                c1 = pl.multiple_of(col_ref[t * groups + g + 1] * order, order)
-                right = jnp.concatenate([omega_buf[pl.ds(c0, order), :], omega_buf[pl.ds(c1, order), :]], axis=0)
-                term = jnp.dot(left, right, preferred_element_type=jnp.float32)
-                total = term if total is None else total + term
-            total = total.astype(jnp.bfloat16)
-            for q in range(chunks):
-                out_ref[q, slot_of[t]] = total[q * rq:(q + 1) * rq]
-
-
-def partials(destination, row_target, col_flat, a_blocks, omega, slots):
-    targets, _, order, _ = a_blocks.shape
-    width = omega.shape[1]
-    dma = pltpu.SemaphoreType.DMA
-    any_space = pl.BlockSpec(memory_space=pl.ANY)
-    return pl.pallas_call(
-        partial_kernel,
-        out_shape=(
-            jax.ShapeDtypeStruct((CHUNKS, slots, order // CHUNKS, width), jnp.bfloat16),
-            jax.ShapeDtypeStruct((slots // CAP, 8, 128), jnp.int32),
-        ),
-        in_specs=[SMEM, SMEM, SMEM, any_space, any_space],
-        out_specs=(VMEM, VMEM),
-        scratch_shapes=[
-            pltpu.VMEM(a_blocks.shape, a_blocks.dtype),
-            pltpu.VMEM(omega.shape, omega.dtype),
-            pltpu.SMEM((targets,), jnp.int32),
-            pltpu.SMEM((slots // CAP,), jnp.int32),
-            dma((targets // LOADS,)), dma((1,)),
-        ],
-        compiler_params=pltpu.CompilerParams(vmem_limit_bytes=40 << 20),
-    )(destination, row_target, col_flat, a_blocks, omega)
-
-
-def greet(nr, nc, r, c):
+def place(dest, target, owners):
+    count = dest.shape[1]
+    i = lax.broadcasted_iota(jnp.int32, (count, count), 0)
+    j = lax.broadcasted_iota(jnp.int32, (count, count), 1)
+    down = jnp.sum(jnp.where(i == j, dest, 0), axis=1, keepdims=True)
+    rank = jnp.sum(jnp.logical_and(down == dest, j < i).astype(jnp.int32), axis=1, keepdims=True)
+    rank_across = jnp.sum(jnp.where(i == j, rank, 0), axis=0, keepdims=True)
+    lane = lax.broadcasted_iota(jnp.int32, (count, 128), 1)
+    which = lax.broadcasted_iota(jnp.int32, (count, 128), 0)
+    source = jnp.sum(jnp.where(down * CAP + rank == lane, which, 0), axis=0, keepdims=True)
+    place_of = lax.broadcasted_iota(jnp.int32, (owners * 8, count), 0)
+    here = place_of == dest * 8 + rank_across
+    rows = jnp.sum(jnp.where(here, target + 1, 0), axis=1, keepdims=True)
+    rows = jnp.where(rows > 0, rows - 1, NOWHERE)
+    return source, jnp.broadcast_to(rows, (owners * 8, 128))
+
+
+def signal_all(nr, nc, r, c):
     barrier = pltpu.get_barrier_semaphore()
     for k in range(1, nr):
         pl.semaphore_signal(barrier, inc=1, device_id=(lax.rem(r + k, nr), c), device_id_type=MESH)
     for k in range(1, nc):
         pl.semaphore_signal(barrier, inc=1, device_id=(r, lax.rem(c + k, nc)), device_id_type=MESH)
-    pl.semaphore_wait(barrier, nr - 1 + nc - 1)
+
+
+def wait_all(nr, nc):
+    pl.semaphore_wait(pltpu.get_barrier_semaphore(), nr - 1 + nc - 1)
+
+
+def greet(nr, nc, r, c):
+    signal_all(nr, nc, r, c)
+    wait_all(nr, nc)
 
 
 def reduce_packed(nr, nc, r, c, gram, landed, cols, full, sems):
@@ -200,15 +155,23 @@
     return jnp.concatenate([order, keep, last, valid], axis=0)
 
 
-def sketch_kernel(nr, nc, send_ref, row_ref, sketch_ref, out_ref, *refs):
-    chunks, _, _, rq, width = send_ref.shape
+def sketch_kernel(nr, nc, dest_hbm, target_hbm, col_hbm, a_hbm, omega_hbm, sketch_ref, out_ref, *refs):
+    chunks = CHUNKS
     gots, refs = refs[:chunks], refs[chunks:]
-    (rows_in, meta, table, prefix, term, to_right, to_left, total, gram, row_s, row_r, own_s,
-     send_s, send_r, right_s, right_r, left_s, left_r), refs = refs[:18], refs[18:]
+    (dest_ref, target_ref, col_ref, a_buf, omega_buf, parts, send_ref, row_ref, sources, a_sem, in_sem,
+     rows_in, meta, table, prefix, term, to_right, to_left, total, gram, row_s, row_r, own_s,
+     send_s, send_r, right_s, right_r, left_s, left_r), refs = refs[:29], refs[29:]
+    targets, groups, order, _ = a_buf.shape
+    rq, width = order // chunks, omega_buf.shape[2]
     slots = nr * CAP
     blocks = nc * RB_DEV
+    loads = targets // LOADS
     r = lax.axis_index("row")
     c = lax.axis_index("col")
+
+    def fetch(i):
+        part = pl.ds(i * LOADS, LOADS)
+        return pltpu.make_async_copy(a_hbm.at[part], a_buf.at[part], a_sem.at[i])
 
     def route(k):
         d = lax.rem(r + k, nr)
@@ -234,20 +197,57 @@
             to_left.at[q, d], to_left.at[q, d], left_s.at[q, d], left_r.at[q, d],
             device_id=(r, lax.rem(c + nc - 1, nc)), device_id_type=MESH)
 
-    for q in range(chunks):
-        keep_own(q).start()
+    others = [pltpu.make_async_copy(src, dst, in_sem.at[i]) for i, (src, dst) in enumerate(
+        ((dest_hbm, dest_ref), (target_hbm, target_ref), (col_hbm, col_ref), (omega_hbm, omega_buf)))]
+    for copy in others:
+        copy.start()
+    for i in range(loads):
+        fetch(i).start()
+    signal_all(nr, nc, r, c)
+    others[0].wait()
+    others[1].wait()
+    source, rows = place(dest_ref[...], target_ref[...], nr)
+    row_ref[...] = rows.reshape(nr, 8, 128)
+    meta[...] = jnp.zeros_like(meta)
+    meta[:1, :] = source
+    to_sources = pltpu.make_async_copy(meta, sources, own_s.at[chunks + 1])
+    to_sources.start()
     own_rows = pltpu.make_async_copy(row_ref.at[r], rows_in.at[r], own_s.at[chunks])
     own_rows.start()
-    greet(nr, nc, r, c)
+    gram[...] = jnp.zeros_like(gram)
+    to_sources.wait()
+    wait_all(nr, nc)
     for k in range(1, nr):
         route(k).start()
-    for k in range(1, nr):
-        swap(0, k).start()
-    gram[...] = jnp.zeros_like(gram)
     own_rows.wait()
+    others[2].wait()
+    others[3].wait()
+
+    @pl.loop(0, loads)
+    def _(i):
+        fetch(i).wait()
+        for local in range(LOADS):
+            t = i * LOADS + local
+            sums = None
+            for g in range(0, groups, 2):
+                left = jnp.concatenate([a_buf[t, g], a_buf[t, g + 1]], axis=1)
+                right = jnp.concatenate([omega_buf[col_ref[g, t]], omega_buf[col_ref[g + 1, t]]], axis=0)
+                product = jnp.dot(left, right, preferred_element_type=jnp.float32)
+                sums = product if sums is None else sums + product
+            sums = sums.astype(jnp.bfloat16)
+            for q in range(chunks):
+                parts[q, t] = sums[q * rq:(q + 1) * rq]
+
+    for q in range(chunks):
+        for d in range(nr):
+            for k in range(CAP):
+                send_ref[q, d, k] = parts[q, sources[0, d * CAP + k]]
+        keep_own(q).start()
+        if q == 0:
+            for k in range(1, nr):
+                swap(0, k).start()
     for k in range(1, nr):
         route(k).wait_recv()
-    meta[...] = jnp.zeros_like(meta)
     meta[:4, :] = arrange(rows_in[...].reshape(nr * 8, 128), slots)
     to_table = pltpu.make_async_copy(meta, table, own_s.at[chunks + 1])
     to_table.start()
@@ -256,10 +256,12 @@
     def collect(q):
         keep_own(q).wait()
         for k in range(1, nr):
-            swap(q, k).wait_recv()
+            swap(q, k).wait_send()
         if q + 1 < chunks:
             for k in range(1, nr):
                 swap(q + 1, k).start()
+        for k in range(1, nr):
+            swap(q, k).wait_recv()
         got = gots[q]
 
         def add(k, acc):
@@ -276,12 +278,18 @@
         @pl.when(c == 0)
         def _():
             for d in range(nc - 1, 0, -1):
+                n = q * (nc - 1) + nc - 1 - d - WINDOW
+                if n >= 0:
+                    hop_right(n // (nc - 1), nc - 1 - n % (nc - 1)).wait_send()
                 to_right[q, d] = term[q % 2, d * RB_DEV:(d + 1) * RB_DEV].astype(jnp.bfloat16)
                 hop_right(q, d).start()
 
         @pl.when(c == nc - 1)
         def _():
             for d in range(nc - 1):
+                n = q * (nc - 1) + d - WINDOW
+                if n >= 0:
+                    hop_left(n // (nc - 1), n % (nc - 1)).wait_send()
                 to_left[q, d] = term[q % 2, d * RB_DEV:(d + 1) * RB_DEV].astype(jnp.bfloat16)
                 hop_left(q, d).start()
 
@@ -329,33 +337,55 @@
     sum_gram(nr, nc, r, c, gram, out_ref, *refs[:4], refs[4:])
     for k in range(1, nr):
         route(k).wait_send()
+
+    @pl.when(c == 0)
+    def _():
+        for n in range(chunks * (nc - 1) - WINDOW, chunks * (nc - 1)):
+            hop_right(n // (nc - 1), nc - 1 - n % (nc - 1)).wait_send()
+
+    @pl.when(c == nc - 1)
+    def _():
+        for n in range(chunks * (nc - 1) - WINDOW, chunks * (nc - 1)):
+            hop_left(n // (nc - 1), n % (nc - 1)).wait_send()
+
     for q in range(chunks):
-        for k in range(1, nr):
-            swap(q, k).wait_send()
         for k in range(1, nc):
-            @pl.when(c + k < nc)
+            @pl.when(jnp.logical_and(c > 0, c + k < nc))
             def _():
                 hop_right(q, c + k).wait_send()
 
-            @pl.when(c - k >= 0)
+            @pl.when(jnp.logical_and(c < nc - 1, c - k >= 0))
             def _():
                 hop_left(q, c - k).wait_send()
 
 
-def make_sketch(send, rows, nr, nc):
-    chunks, _, _, rq, width = send.shape
+def make_sketch(dest, target, col_target, a_blocks, omega, nr, nc):
+    targets, _, order, _ = a_blocks.shape
+    width = omega.shape[2]
+    chunks, rq = CHUNKS, order // CHUNKS
     dma = pltpu.SemaphoreType.DMA
     slots, blocks = nr * CAP, nc * RB_DEV
     hops = pltpu.VMEM((chunks, nc, RB_DEV, rq, width), jnp.bfloat16)
+    hbm = pl.BlockSpec(memory_space=pltpu.HBM)
     return pl.pallas_call(
         functools.partial(sketch_kernel, nr, nc),
         out_shape=(
-            jax.ShapeDtypeStruct((RB_DEV * chunks * rq, width), jnp.float32),
+            jax.ShapeDtypeStruct((RB_DEV * order, width), jnp.float32),
             jax.ShapeDtypeStruct((width, width), jnp.float32),
         ),
-        in_specs=[VMEM, VMEM],
+        in_specs=[hbm] * 5,
         out_specs=(VMEM, VMEM),
         scratch_shapes=[pltpu.VMEM((slots, rq, width), jnp.bfloat16)] * chunks + [
+            pltpu.VMEM(dest.shape, jnp.int32),
+            pltpu.VMEM(target.shape, jnp.int32),
+            pltpu.SMEM(col_target.shape, jnp.int32),
+            pltpu.VMEM(a_blocks.shape, a_blocks.dtype),
+            pltpu.VMEM(omega.shape, omega.dtype),
+            pltpu.VMEM((chunks, targets, rq, width), jnp.bfloat16),
+            pltpu.VMEM((chunks, nr, CAP, rq, width), jnp.bfloat16),
+            pltpu.VMEM((nr, 8, 128), jnp.int32),
+            pltpu.SMEM((8, 128), jnp.int32),
+            dma((targets // LOADS,)), dma((4,)),
             pltpu.VMEM((nr, 8, 128), jnp.int32),
             pltpu.VMEM((8, 128), jnp.int32),
             pltpu.SMEM((8, 128), jnp.int32),
@@ -368,8 +398,8 @@
             dma((chunks, nr)), dma((chunks, nr)),
             dma((chunks, nc)), dma((chunks, nc)), dma((chunks, nc)), dma((chunks, nc)),
         ] + packed_scratch(nr, nc, width),
-        compiler_params=pltpu.CompilerParams(collective_id=1, has_side_effects=True, vmem_limit_bytes=32 << 20),
-    )(send, rows)
+        compiler_params=pltpu.CompilerParams(collective_id=1, has_side_effects=True, vmem_limit_bytes=60 << 20),
+    )(dest, target, col_target, a_blocks, omega)
 
 
 def gram_sum_kernel(nr, nc, gram, out_ref, packed, landed, cols, full, *sems):
@@ -458,8 +488,51 @@
             work[...] = jnp.where(below, work[...] - update, work[...])
 
 
-def first_kernel(gram, sketch, upper, once, second, work, inverse):
-    factor_gram(gram, work, upper, inverse)
+def factor_kernel(scale, gram, upper_out, factor, inverse, again, work):
+    factor_gram(gram, work, upper_out, inverse)
+    factor[...] = upper_out[...] * (1.0 / scale)
+    order = gram.shape[0]
+    row = lax.broadcasted_iota(jnp.int32, (order, order), 0)
+    col = lax.broadcasted_iota(jnp.int32, (order, order), 1)
+    diag = jnp.sum(jnp.where(row == col, gram[...], 0.0), axis=0, keepdims=True)
+    spread = jnp.sum(inverse[...] * inverse[...], axis=0, keepdims=True) * diag
+    mean = jnp.sum(spread) * (1.0 / order)
+    again[0] = jnp.where(mean <= INFLATION, 0, 1)
+
+
+def factor_first(gram, scale):
+    order = gram.shape[0]
+    square = jax.ShapeDtypeStruct((order, order), jnp.float32)
+    return pl.pallas_call(
+        functools.partial(factor_kernel, scale),
+        out_shape=(square, square, square, jax.ShapeDtypeStruct((1,), jnp.int32)),
+        in_specs=[VMEM],
+        out_specs=(VMEM, VMEM, VMEM, SMEM),
+        scratch_shapes=[pltpu.VMEM((order, 2 * order), jnp.float32)],
+        compiler_params=pltpu.CompilerParams(vmem_limit_bytes=16 << 20),
+    )(gram)
+
+
+def apply_kernel(scale, inverse, sketch, basis):
+    step = 256
+
+    @pl.loop(0, sketch.shape[0] // step)
+    def _(i):
+        part = pl.ds(pl.multiple_of(i * step, step), step)
+        basis[part, :] = dot_nt(sketch[part, :], inverse[...]) * scale
+
+
+def apply_inverse(inverse, sketch, scale):
+    return pl.pallas_call(
+        functools.partial(apply_kernel, scale),
+        out_shape=jax.ShapeDtypeStruct(sketch.shape, jnp.float32),
+        in_specs=[VMEM, VMEM],
+        out_specs=VMEM,
+        compiler_params=pltpu.CompilerParams(vmem_limit_bytes=16 << 20),
+    )(inverse, sketch)
+
+
+def once_kernel(inverse, sketch, once, second):
     second[...] = jnp.zeros_like(second)
     step = 256
 
@@ -471,17 +544,17 @@
         second[...] += dot_tn(rows, rows)
 
 
-def first_pass(gram, sketch):
-    order = gram.shape[0]
-    square = jax.ShapeDtypeStruct((order, order), jnp.float32)
+def once_pass(inverse, sketch):
     return pl.pallas_call(
-        first_kernel,
-        out_shape=(square, jax.ShapeDtypeStruct(sketch.shape, jnp.float32), square),
+        once_kernel,
+        out_shape=(
+            jax.ShapeDtypeStruct(sketch.shape, jnp.float32),
+            jax.ShapeDtypeStruct(inverse.shape, jnp.float32),
+        ),
         in_specs=[VMEM, VMEM],
-        out_specs=(VMEM, VMEM, VMEM),
-        scratch_shapes=[pltpu.VMEM((order, 2 * order), jnp.float32), pltpu.VMEM((order, order), jnp.float32)],
+        out_specs=(VMEM, VMEM),
         compiler_params=pltpu.CompilerParams(vmem_limit_bytes=16 << 20),
-    )(gram, sketch)
+    )(inverse, sketch)
 
 
 def last_kernel(scale, gram, once, upper_one, basis, factor, work, upper, inverse):
@@ -513,15 +586,19 @@
 
 def body(nr, nc, a_blocks, omega, route_dest, row_target, col_target):
     order = a_blocks.shape[2]
-    width = omega.shape[1]
-    slots = nr * CAP
-    send, rows = partials(route_dest.reshape(-1), row_target, col_target.reshape(-1), a_blocks, omega, slots)
-    send = send.reshape(CHUNKS, nr, CAP, order // CHUNKS, width)
-    sketch, gram_one = make_sketch(send, rows, nr, nc)
-    upper_one, once, gram_part = first_pass(gram_one, sketch)
-    gram_two = gram_sum(gram_part, nr, nc)
+    sketch, gram_one = make_sketch(
+        route_dest.T, row_target.reshape(1, -1), col_target.T, a_blocks, omega.reshape(-1, order, omega.shape[1]), nr, nc)
     scale = float(nr * nc * RB_DEV * order) ** 0.5
-    return last_pass(gram_two, once, upper_one, scale)
+    upper, factor, inverse, again = factor_first(gram_one, scale)
+
+    def orthogonalize_again():
+        once, gram_part = once_pass(inverse, sketch)
+        return last_pass(gram_sum(gram_part, nr, nc), once, upper, scale)
+
+    def keep_once():
+        return apply_inverse(inverse, sketch, scale), factor
+
+    return lax.cond(again[0] != 0, orthogonalize_again, keep_once)
 
 
 def solution(mesh):

time: 137 us -> 119 us (0.87)
  Pallas kernels: 132 us -> 116 us
  local copies, waits for them, and re-layouts: 3.76 us -> 0.94 us
    pallas_call x4 -> x2, Pallas kernels: 58.4 us -> 17.7 us  [the longest x1 15.1 us: factor_first(): pl.pallas_call(functools.partial(factor_kernel, scale), out_shape=(square...]
    pallas_call x1, Pallas kernels: 73.8 us -> 98.5 us  [make_sketch(): pl.pallas_call(functools.partial(sketch_kernel, nr, nc), out_shape=(jax.S...]
    unnamed x7 -> x2, local copies, waits for them, and re-layouts: 3.68 us -> 0.94 us
where the time goes in v2:
time: 119 us
  Pallas kernels  116 us (97%)
  between operations  1.3 us (1%)
    pallas_call x1, Pallas kernels, make_sketch(): pl.pallas_call(functools.partial(sketch_kernel, nr, nc), out_shape=(jax.S...  98.5 us
    pallas_call x1, Pallas kernels, factor_first(): pl.pallas_call(functools.partial(factor_kernel, scale), out_shape=(square...  15.1 us
    pallas_call x1, Pallas kernels, apply_inverse(): pl.pallas_call(functools.partial(apply_kernel, scale), out_shape=jax.Shap...  2.64 us

profile of v2, /device:TPU:0, one launch (start us, length us, event | category | flops | bytes accessed | tf_op | source)
XLA Modules:
  0.0 118.5 jit_solution(5363130096981687161)
XLA Ops:
  0.6 98.5 %shard_map.70 = (f32[1024,256]{1,0:T(8,128)S(1)}, f32[256,256]{1,0:T(8,128)}) custom-call(s32[1,32]{1,0:T(1,128)} %bitcast.7, s32[1,32]{1,0:T(1,128)} %bitcast.8, s32[16,32]{1,0:T(8,128)} %bitcast.6, bf16[32,16,128,128]{3,2,1,0:T(8,128)(2,1)} %a_hbm.1, bf16[32,128,256]{2,1,0:T(8,128)(2,1)} %bitcast.5), custom_call_target="tpu_custom_call" | custom-call | tf_op jit(solution)/shard_map/pallas_call | solution.py:370
  99.2 0.0 copy-start
  99.2 0.9 copy-done
  100.1 15.1 %shard_map.71 = (f32[256,256]{1,0:T(8,128)S(1)}, f32[256,256]{1,0:T(8,128)}, f32[256,256]{1,0:T(8,128)S(1)}, s32[1]{0:T(128)}) custom-call(f32[256,256]{1,0:T(8,128)S(1)} %copy-done), custom_call_target="tpu_custom_call" | custom-call | tf_op jit(solution)/shard_map/pallas_call | solution.py:506
  115.9 2.7 %conditional.1 = (f32[256,256]{1,0:T(8,128)}, f32[1024,256]{1,0:T(8,128)}) conditional(s32[]{:T(128)} %bitcast.4, (f32[256,256]{1,0:T(8,128)S(1)}, f32[1024,256]{1,0:T(8,128)S(1)}, f32[256,256]{1,0:T(8,128)}) %tuple.14, (f32[256,256]{1,0:T(8,128)S(1)}, f32[1024,256]{1,0:T(8,128)S(1)}, f32[256,256]{1,0:T(8,128)S(1)}) %tuple.15), branch_computations={%region_0.0_spmd, %region_1.0_spmd} | conditional | bytes 16 | solution.py:601
  115.9 2.6 %branch_0_fun.1 = f32[1024,256]{1,0:T(8,128)} custom-call(f32[256,256]{1,0:T(8,128)S(1)} %get-tuple-element.12.inverse, f32[1024,256]{1,0:T(8,128)S(1)} %get-tuple-element.13.sketch), custom_call_target="tpu_custom_call" | custom-call | tf_op jit(solution)/shard_map/cond/branch_0_fun/pallas_call | solution.py:526
Async XLA Ops:
  99.2 1.0 copy-start

commit v3 on v2

--- a/solution.py
+++ b/solution.py
@@ -10,11 +10,12 @@
 RB_DEV = 8
 CAP = 4
 PANEL = 64
-LOADS = 4
+LOADS = 8
 NOWHERE = 1 << 20
 INFLATION = 2.0
 CHUNKS = 8
 WINDOW = 2
+TERMS = 4
 WIDE = 4
 MESH = pl.DeviceIdType.MESH
 VMEM = pl.BlockSpec(memory_space=pltpu.VMEM)
@@ -215,16 +216,10 @@
     own_rows = pltpu.make_async_copy(row_ref.at[r], rows_in.at[r], own_s.at[chunks])
     own_rows.start()
     gram[...] = jnp.zeros_like(gram)
-    to_sources.wait()
-    wait_all(nr, nc)
-    for k in range(1, nr):
-        route(k).start()
-    own_rows.wait()
     others[2].wait()
     others[3].wait()
 
-    @pl.loop(0, loads)
-    def _(i):
+    def multiply(i, carry):
         fetch(i).wait()
         for local in range(LOADS):
             t = i * LOADS + local
@@ -237,7 +232,15 @@
             sums = sums.astype(jnp.bfloat16)
             for q in range(chunks):
                 parts[q, t] = sums[q * rq:(q + 1) * rq]
-
+        return carry
+
+    lax.fori_loop(0, loads // 2, multiply, 0)
+    wait_all(nr, nc)
+    for k in range(1, nr):
+        route(k).start()
+    lax.fori_loop(loads // 2, loads, multiply, 0)
+    own_rows.wait()
+    to_sources.wait()
     for q in range(chunks):
         for d in range(nr):
             for k in range(CAP):
@@ -269,11 +272,11 @@
             prefix[k] = acc
             return acc
 
-        lax.fori_loop(0, slots, add, jnp.zeros((rq, width), jnp.float32), unroll=4)
-
-        @pl.loop(0, blocks, unroll=4)
+        lax.fori_loop(0, slots, add, jnp.zeros((rq, width), jnp.float32), unroll=8)
+
+        @pl.loop(0, blocks, unroll=8)
         def _(b):
-            term[q % 2, b] = prefix[table[2, b]] * table[3, b].astype(jnp.float32)
+            term[q % TERMS, b] = prefix[table[2, b]] * table[3, b].astype(jnp.float32)
 
         @pl.when(c == 0)
         def _():
@@ -281,7 +284,7 @@
                 n = q * (nc - 1) + nc - 1 - d - WINDOW
                 if n >= 0:
                     hop_right(n // (nc - 1), nc - 1 - n % (nc - 1)).wait_send()
-                to_right[q, d] = term[q % 2, d * RB_DEV:(d + 1) * RB_DEV].astype(jnp.bfloat16)
+                to_right[q, d] = term[q % TERMS, d * RB_DEV:(d + 1) * RB_DEV].astype(jnp.bfloat16)
                 hop_right(q, d).start()
 
         @pl.when(c == nc - 1)
@@ -290,7 +293,7 @@
                 n = q * (nc - 1) + d - WINDOW
                 if n >= 0:
                     hop_left(n // (nc - 1), n % (nc - 1)).wait_send()
-                to_left[q, d] = term[q % 2, d * RB_DEV:(d + 1) * RB_DEV].astype(jnp.bfloat16)
+                to_left[q, d] = term[q % TERMS, d * RB_DEV:(d + 1) * RB_DEV].astype(jnp.bfloat16)
                 hop_left(q, d).start()
 
     def pass_on(q):
@@ -299,7 +302,7 @@
             def _():
                 d = c + k
                 hop_right(q, d).wait_recv()
-                mine = term[q % 2, pl.ds(d * RB_DEV, RB_DEV)]
+                mine = term[q % TERMS, pl.ds(d * RB_DEV, RB_DEV)]
                 to_right[q, d] = (to_right[q, d].astype(jnp.float32) + mine).astype(jnp.bfloat16)
                 hop_right(q, d).start()
 
@@ -307,11 +310,13 @@
             def _():
                 d = c - k
                 hop_left(q, d).wait_recv()
-                mine = term[q % 2, pl.ds(d * RB_DEV, RB_DEV)]
+                mine = term[q % TERMS, pl.ds(d * RB_DEV, RB_DEV)]
                 to_left[q, d] = (to_left[q, d].astype(jnp.float32) + mine).astype(jnp.bfloat16)
                 hop_left(q, d).start()
 
-        total[...] = term[q % 2, pl.ds(c * RB_DEV, RB_DEV)]
+
+    def finish(q):
+        total[...] = term[q % TERMS, pl.ds(c * RB_DEV, RB_DEV)]
 
         @pl.when(c > 0)
         def _():
@@ -329,11 +334,13 @@
         rows = total[...].reshape(RB_DEV * rq, width)
         gram[...] += dot_tn(rows, rows)
 
-    for q in range(chunks):
-        collect(q)
-        if q > 0:
+    for q in range(chunks + 2):
+        if q < chunks:
+            collect(q)
+        if 1 <= q <= chunks:
             pass_on(q - 1)
-    pass_on(chunks - 1)
+        if q >= 2:
+            finish(q - 2)
     sum_gram(nr, nc, r, c, gram, out_ref, *refs[:4], refs[4:])
     for k in range(1, nr):
         route(k).wait_send()
@@ -390,7 +397,7 @@
             pltpu.VMEM((8, 128), jnp.int32),
             pltpu.SMEM((8, 128), jnp.int32),
             pltpu.VMEM((slots, rq, width), jnp.float32),
-            pltpu.VMEM((2, blocks, rq, width), jnp.float32),
+            pltpu.VMEM((TERMS, blocks, rq, width), jnp.float32),
             hops, hops,
             pltpu.VMEM((RB_DEV, rq, width), jnp.float32),
             pltpu.VMEM((width, width), jnp.float32),

time: 119 us -> 96.4 us (0.81)
  Pallas kernels: 116 us -> 94 us
    pallas_call x1, Pallas kernels: 98.5 us -> 76.3 us  [make_sketch(): pl.pallas_call(functools.partial(sketch_kernel, nr, nc), out_shape=(jax.S...]
where the time goes in v3:
time: 96.4 us; the launch traced here: 96.2 us
  Pallas kernels  94 us (98%)
  between operations  1.3 us (1%)
    pallas_call x1, Pallas kernels, make_sketch(): pl.pallas_call(functools.partial(sketch_kernel, nr, nc), out_shape=(jax.S...  76.3 us
    pallas_call x1, Pallas kernels, factor_first(): pl.pallas_call(functools.partial(factor_kernel, scale), out_shape=(square...  15.1 us
    pallas_call x1, Pallas kernels, apply_inverse(): pl.pallas_call(functools.partial(apply_kernel, scale), out_shape=jax.Shap...  2.64 us

profile of v3, /device:TPU:0, one launch (start us, length us, event | category | flops | bytes accessed | tf_op | source)
XLA Modules:
  0.0 96.2 jit_solution(228310831146583372)
XLA Ops:
  0.6 76.3 %shard_map.70 = (f32[1024,256]{1,0:T(8,128)S(1)}, f32[256,256]{1,0:T(8,128)}) custom-call(s32[1,32]{1,0:T(1,128)} %bitcast.7, s32[1,32]{1,0:T(1,128)} %bitcast.8, s32[16,32]{1,0:T(8,128)} %bitcast.6, bf16[32,16,128,128]{3,2,1,0:T(8,128)(2,1)} %a_hbm.1, bf16[32,128,256]{2,1,0:T(8,128)(2,1)} %bitcast.5), custom_call_target="tpu_custom_call" | custom-call | tf_op jit(solution)/shard_map/pallas_call | solution.py:377
  76.9 0.0 copy-start
  76.9 0.9 copy-done
  77.8 15.1 %shard_map.71 = (f32[256,256]{1,0:T(8,128)S(1)}, f32[256,256]{1,0:T(8,128)}, f32[256,256]{1,0:T(8,128)S(1)}, s32[1]{0:T(128)}) custom-call(f32[256,256]{1,0:T(8,128)S(1)} %copy-done), custom_call_target="tpu_custom_call" | custom-call | tf_op jit(solution)/shard_map/pallas_call | solution.py:513
  93.6 2.7 %conditional.1 = (f32[256,256]{1,0:T(8,128)}, f32[1024,256]{1,0:T(8,128)}) conditional(s32[]{:T(128)} %bitcast.4, (f32[256,256]{1,0:T(8,128)S(1)}, f32[1024,256]{1,0:T(8,128)S(1)}, f32[256,256]{1,0:T(8,128)}) %tuple.14, (f32[256,256]{1,0:T(8,128)S(1)}, f32[1024,256]{1,0:T(8,128)S(1)}, f32[256,256]{1,0:T(8,128)S(1)}) %tuple.15), branch_computations={%region_0.0_spmd, %region_1.0_spmd} | conditional | bytes 16 | solution.py:608
  93.6 2.6 %branch_0_fun.1 = f32[1024,256]{1,0:T(8,128)} custom-call(f32[256,256]{1,0:T(8,128)S(1)} %get-tuple-element.12.inverse, f32[1024,256]{1,0:T(8,128)S(1)} %get-tuple-element.13.sketch), custom_call_target="tpu_custom_call" | custom-call | tf_op jit(solution)/shard_map/cond/branch_0_fun/pallas_call | solution.py:533
Async XLA Ops:
  76.9 1.0 copy-start

commit v4 on v3

--- a/solution.py
+++ b/solution.py
@@ -16,7 +16,6 @@
 CHUNKS = 8
 WINDOW = 2
 TERMS = 4
-WIDE = 4
 MESH = pl.DeviceIdType.MESH
 VMEM = pl.BlockSpec(memory_space=pltpu.VMEM)
 SMEM = pl.BlockSpec(memory_space=pltpu.SMEM)
@@ -123,17 +122,18 @@
     ]
 
 
-def sum_gram(nr, nc, r, c, gram, out_ref, packed, landed, cols, full, sems):
+def sum_gram(nr, nc, r, c, gram, out_ref, packed, landed, cols, full, *sems):
     half = gram.shape[0] // 2
     packed[:half, :] = gram[:half, :half]
     packed[half:2 * half, :] = gram[:half, half:]
     packed[2 * half:, :] = gram[half:, half:]
     reduce_packed(nr, nc, r, c, packed, landed, cols, full, sems)
-    out_ref[:half, :half] = full[:half, :]
-    side = full[half:2 * half, :]
+    whole = full[...]
+    out_ref[:half, :half] = whole[:half]
+    side = whole[half:2 * half]
     out_ref[:half, half:] = side
     out_ref[half:, :half] = side.T
-    out_ref[half:, half:] = full[2 * half:, :]
+    out_ref[half:, half:] = whole[2 * half:]
 
 
 def arrange(rows, slots):
@@ -156,7 +156,7 @@
     return jnp.concatenate([order, keep, last, valid], axis=0)
 
 
-def sketch_kernel(nr, nc, dest_hbm, target_hbm, col_hbm, a_hbm, omega_hbm, sketch_ref, out_ref, *refs):
+def sketch_kernel(nr, nc, dest_hbm, target_hbm, col_hbm, a_hbm, omega_hbm, sketch_ref, *refs):
     chunks = CHUNKS
     gots, refs = refs[:chunks], refs[chunks:]
     (dest_ref, target_ref, col_ref, a_buf, omega_buf, parts, send_ref, row_ref, sources, a_sem, in_sem,
@@ -341,7 +341,7 @@
             pass_on(q - 1)
         if q >= 2:
             finish(q - 2)
-    sum_gram(nr, nc, r, c, gram, out_ref, *refs[:4], refs[4:])
+    sum_gram(nr, nc, r, c, gram, sketch_ref.at[pl.ds(RB_DEV * order, width)], *refs)
     for k in range(1, nr):
         route(k).wait_send()
 
@@ -376,12 +376,9 @@
     hbm = pl.BlockSpec(memory_space=pltpu.HBM)
     return pl.pallas_call(
         functools.partial(sketch_kernel, nr, nc),
-        out_shape=(
-            jax.ShapeDtypeStruct((RB_DEV * order, width), jnp.float32),
-            jax.ShapeDtypeStruct((width, width), jnp.float32),
-        ),
+        out_shape=jax.ShapeDtypeStruct((RB_DEV * order + width, width), jnp.float32),
         in_specs=[hbm] * 5,
-        out_specs=(VMEM, VMEM),
+        out_specs=VMEM,
         scratch_shapes=[pltpu.VMEM((slots, rq, width), jnp.bfloat16)] * chunks + [
             pltpu.VMEM(dest.shape, jnp.int32),
             pltpu.VMEM(target.shape, jnp.int32),
@@ -409,11 +406,11 @@
     )(dest, target, col_target, a_blocks, omega)
 
 
-def gram_sum_kernel(nr, nc, gram, out_ref, packed, landed, cols, full, *sems):
+def gram_sum_kernel(nr, nc, gram, out_ref, *refs):
     r = lax.axis_index("row")
     c = lax.axis_index("col")
     greet(nr, nc, r, c)
-    sum_gram(nr, nc, r, c, gram, out_ref, packed, landed, cols, full, sems)
+    sum_gram(nr, nc, r, c, gram, out_ref, *refs)
 
 
 def gram_sum(gram, nr, nc):
@@ -432,73 +429,77 @@
     shape = (8, x.shape[1])
     groups = [x[i:i + 8, :] for i in range(0, rows, 8)]
     sub = lax.broadcasted_iota(jnp.int32, shape, 0)
-    for j in range(0, rows, WIDE):
-        g, o = divmod(j, 8)
-        cols = [[jnp.broadcast_to(groups[i][:, j + l:j + l + 1], shape) for l in range(WIDE)]
+    for g in range(rows // 8):
+        j = 8 * g
+        cols = [[jnp.broadcast_to(groups[i][:, j + l:j + l + 1], shape) for l in range(8)]
                 for i in range(g, rows // 8)]
-        piv = [[jnp.broadcast_to(cols[0][l][o + k:o + k + 1, :], shape) for l in range(WIDE)] for k in range(WIDE)]
-        tops = [jnp.broadcast_to(groups[g][o + k:o + k + 1, :], shape) for k in range(WIDE)]
+        piv = [[jnp.broadcast_to(cols[0][l][k:k + 1, :], shape) for l in range(8)] for k in range(8)]
+        tops = [jnp.broadcast_to(groups[g][k:k + 1, :], shape) for k in range(8)]
         recip = []
-        for k in range(WIDE):
-            recip.append(1.0 / piv[k][k])
-            for m in range(k + 1, WIDE):
+        for k in range(8):
+            if k % 2 == 0:
+                det = piv[k][k] * piv[k + 1][k + 1] - piv[k + 1][k] * piv[k][k + 1]
+                recip += [1.0 / piv[k][k], piv[k][k] * (1.0 / det)]
+            for m in range(k + 1, 8):
                 q = piv[m][k] * recip[k]
-                for l in range(k + 1, WIDE):
+                for l in range(k + 1, 8):
                     piv[m][l] = piv[m][l] - q * piv[k][l]
                 tops[m] = tops[m] - q * tops[k]
-        for i in range(g, rows // 8):
+        for i in range(g + 1, rows // 8):
             here = cols[i - g]
             value = groups[i]
-            for k in range(WIDE):
+            for k in range(8):
                 f = here[k] * recip[k]
-                for l in range(k + 1, WIDE):
+                for l in range(k + 1, 8):
                     here[l] = here[l] - f * piv[k][l]
                 value = value - f * tops[k]
-            if i == g:
-                value = jnp.where(sub >= o + WIDE, value, groups[i])
-                for k in range(1, WIDE):
-                    value = jnp.where(sub == o + k, tops[k], value)
             groups[i] = value
+        for k in range(1, 8):
+            groups[g] = jnp.where(sub == k, tops[k], groups[g])
     return jnp.concatenate(groups, axis=0)
 
 
-def factor_gram(gram, work, upper, inverse):
+def factor_gram(gram, left, right, upper, inverse):
     order = gram.shape[0]
     row = lax.broadcasted_iota(jnp.int32, (order, order), 0)
     col = lax.broadcasted_iota(jnp.int32, (order, order), 1)
-    work[:, :order] = gram[...]
-    work[:, order:] = (row == col).astype(jnp.float32)
+    only = jnp.where(row == col, gram[...], 0.0)
+    diag = jnp.sum(only, axis=0, keepdims=True)
+    unit = 1.0 / jnp.sqrt(diag)
+    back = diag * unit
+    left[...] = gram[...] * (1.0 / jnp.sqrt(jnp.sum(only, axis=1, keepdims=True))) * unit
+    right[...] = jnp.where(row == col, unit, 0.0)
+    upper[...] = jnp.zeros_like(upper)
+    inverse[...] = jnp.zeros_like(inverse)
     lane = lax.broadcasted_iota(jnp.int32, (PANEL, 2 * PANEL), 1)
     prow = lax.broadcasted_iota(jnp.int32, (PANEL, 2 * PANEL), 0)
-
-    @pl.loop(0, order // PANEL)
-    def _(p):
-        base = pl.multiple_of(p * PANEL, PANEL)
-        tile = work[pl.ds(base, PANEL), pl.ds(pl.multiple_of((p // 2) * 2 * PANEL, 2 * PANEL), 2 * PANEL)]
-        tile = jnp.where(p % 2 == 1, pltpu.roll(tile, PANEL, 1), tile)
-        x = jnp.where(lane < PANEL, tile, (lane - PANEL == prow).astype(jnp.float32))
-        x = eliminate(x)
-        diag = jnp.sum(jnp.where(lane == prow, x, 0.0), axis=1, keepdims=True)
-        left = pltpu.roll(x, PANEL, 1)[:, :PANEL]
-        panel = dot_nn(left, work[pl.ds(base, PANEL), :])
-        root = 1.0 / jnp.sqrt(diag)
-        pcol = lax.broadcasted_iota(jnp.int32, (PANEL, order), 1)
-        pr = lax.broadcasted_iota(jnp.int32, (PANEL, order), 0) + base
-        upper[pl.ds(base, PANEL), :] = jnp.where(pcol >= pr, panel[:, :order] * root, 0.0)
-        inverse[pl.ds(base, PANEL), :] = jnp.where(pcol <= pr, panel[:, order:] * root, 0.0)
-
-        @pl.when(p < order // PANEL - 1)
-        def _():
-            half = panel * root
-            update = dot_tn(half[:, :order], half)
-            below = lax.broadcasted_iota(jnp.int32, (order, 1), 0) >= base + PANEL
-            work[...] = jnp.where(below, work[...] - update, work[...])
-
-
-def factor_kernel(scale, gram, upper_out, factor, inverse, again, work):
-    factor_gram(gram, work, upper_out, inverse)
+    for base in range(0, order, PANEL):
+        low = base // (2 * PANEL) * 2 * PANEL
+        high = low + 2 * PANEL
+        here = slice(base, base + PANEL)
+        tile = left[here, low:high]
+        if base > low:
+            tile = pltpu.roll(tile, PANEL, 1)
+        x = eliminate(jnp.where(lane < PANEL, tile, (lane - PANEL == prow).astype(jnp.float32)))
+        root = 1.0 / jnp.sqrt(jnp.sum(jnp.where(lane == prow, x, 0.0), axis=1, keepdims=True))
+        factor = pltpu.roll(x, PANEL, 1)[:, :PANEL]
+        u = dot_nn(factor, left[here, low:]) * root
+        v = dot_nn(factor, right[here, :high]) * root
+        upper[here, low:] = jnp.where(col[here, low:] >= row[here, low:], u * back[:, low:], 0.0)
+        inverse[here, :high] = jnp.where(col[here, :high] <= row[here, :high], v, 0.0)
+        after = base + PANEL
+        if after < order:
+            start = after // (2 * PANEL) * 2 * PANEL
+            rest = u[:, start - low:]
+            left[after:, start:] -= dot_tn(rest, rest)[after - start:]
+            right[after:, :high] -= dot_tn(rest, v)[after - start:]
+
+
+def factor_kernel(scale, sketch, upper_out, factor, inverse, again, left, right):
+    order = inverse.shape[0]
+    gram = sketch.at[pl.ds(sketch.shape[0] - order, order)]
+    factor_gram(gram, left, right, upper_out, inverse)
     factor[...] = upper_out[...] * (1.0 / scale)
-    order = gram.shape[0]
     row = lax.broadcasted_iota(jnp.int32, (order, order), 0)
     col = lax.broadcasted_iota(jnp.int32, (order, order), 1)
     diag = jnp.sum(jnp.where(row == col, gram[...], 0.0), axis=0, keepdims=True)
@@ -507,34 +508,42 @@
     again[0] = jnp.where(mean <= INFLATION, 0, 1)
 
 
-def factor_first(gram, scale):
-    order = gram.shape[0]
+def factor_first(sketch, scale):
+    order = sketch.shape[1]
     square = jax.ShapeDtypeStruct((order, order), jnp.float32)
     return pl.pallas_call(
         functools.partial(factor_kernel, scale),
         out_shape=(square, square, square, jax.ShapeDtypeStruct((1,), jnp.int32)),
         in_specs=[VMEM],
         out_specs=(VMEM, VMEM, VMEM, SMEM),
-        scratch_shapes=[pltpu.VMEM((order, 2 * order), jnp.float32)],
+        scratch_shapes=[pltpu.VMEM((order, order), jnp.float32)] * 2,
         compiler_params=pltpu.CompilerParams(vmem_limit_bytes=16 << 20),
-    )(gram)
-
-
-def apply_kernel(scale, inverse, sketch, basis):
-    step = 256
-
-    @pl.loop(0, sketch.shape[0] // step)
-    def _(i):
-        part = pl.ds(pl.multiple_of(i * step, step), step)
-        basis[part, :] = dot_nt(sketch[part, :], inverse[...]) * scale
+    )(sketch)
+
+
+def apply_kernel(scale, inverse, sketch, basis, ready, sem):
+    pieces, step, _ = ready.shape
+    matrix = inverse[...] * scale
+
+    def store(i):
+        return pltpu.make_async_copy(ready.at[i], basis.at[pl.ds(i * step, step)], sem.at[i])
+
+    for i in range(pieces):
+        ready[i] = dot_nt(sketch[i * step:(i + 1) * step, :], matrix)
+        store(i).start()
+    for i in range(pieces):
+        store(i).wait()
 
 
 def apply_inverse(inverse, sketch, scale):
+    rows, width = sketch.shape[0] - sketch.shape[1], sketch.shape[1]
+    pieces = 4
     return pl.pallas_call(
         functools.partial(apply_kernel, scale),
-        out_shape=jax.ShapeDtypeStruct(sketch.shape, jnp.float32),
+        out_shape=jax.ShapeDtypeStruct((rows, width), jnp.float32),
         in_specs=[VMEM, VMEM],
-        out_specs=VMEM,
+        out_specs=pl.BlockSpec(memory_space=pltpu.HBM),
+        scratch_shapes=[pltpu.VMEM((pieces, rows // pieces, width), jnp.float32), pltpu.SemaphoreType.DMA((pieces,))],
         compiler_params=pltpu.CompilerParams(vmem_limit_bytes=16 << 20),
     )(inverse, sketch)
 
@@ -543,7 +552,7 @@
     second[...] = jnp.zeros_like(second)
     step = 256
 
-    @pl.loop(0, sketch.shape[0] // step)
+    @pl.loop(0, once.shape[0] // step)
     def _(i):
         part = pl.ds(pl.multiple_of(i * step, step), step)
         rows = dot_nt(sketch[part, :], inverse[...])
@@ -555,7 +564,7 @@
     return pl.pallas_call(
         once_kernel,
         out_shape=(
-            jax.ShapeDtypeStruct(sketch.shape, jnp.float32),
+            jax.ShapeDtypeStruct((sketch.shape[0] - sketch.shape[1], sketch.shape[1]), jnp.float32),
             jax.ShapeDtypeStruct(inverse.shape, jnp.float32),
         ),
         in_specs=[VMEM, VMEM],
@@ -564,8 +573,8 @@
     )(inverse, sketch)
 
 
-def last_kernel(scale, gram, once, upper_one, basis, factor, work, upper, inverse):
-    factor_gram(gram, work, upper, inverse)
+def last_kernel(scale, gram, once, upper_one, basis, factor, left, right, upper, inverse):
+    factor_gram(gram, left, right, upper, inverse)
     factor[...] = dot_nn(upper[...], upper_one[...]) * (1.0 / scale)
     step = 256
 
@@ -586,17 +595,17 @@
         ),
         in_specs=[VMEM, VMEM, VMEM],
         out_specs=(VMEM, VMEM),
-        scratch_shapes=[pltpu.VMEM((order, 2 * order), jnp.float32), square, square],
+        scratch_shapes=[square] * 4,
         compiler_params=pltpu.CompilerParams(vmem_limit_bytes=16 << 20),
     )(gram, once, upper_one)
 
 
 def body(nr, nc, a_blocks, omega, route_dest, row_target, col_target):
     order = a_blocks.shape[2]
-    sketch, gram_one = make_sketch(
+    sketch = make_sketch(
         route_dest.T, row_target.reshape(1, -1), col_target.T, a_blocks, omega.reshape(-1, order, omega.shape[1]), nr, nc)
     scale = float(nr * nc * RB_DEV * order) ** 0.5
-    upper, factor, inverse, again = factor_first(gram_one, scale)
+    upper, factor, inverse, again = factor_first(sketch, scale)
 
     def orthogonalize_again():
         once, gram_part = once_pass(inverse, sketch)

time: 96.4 us -> 90.7 us (0.941)
  Pallas kernels: 94 us -> 88.8 us
    pallas_call x1, Pallas kernels: 15.1 us -> 11.2 us  [factor_first(): pl.pallas_call(functools.partial(factor_kernel, scale), out_shape=(square...]
where the time goes in v4:
time: 90.7 us; the launch traced here: 90.5 us
  Pallas kernels  88.8 us (98%)
  between operations  1.48 us (2%)
    pallas_call x1, Pallas kernels, make_sketch(): pl.pallas_call(functools.partial(sketch_kernel, nr, nc), out_shape=jax.Sh...  75.7 us
    pallas_call x1, Pallas kernels, factor_first(): pl.pallas_call(functools.partial(factor_kernel, scale), out_shape=(square...  11.2 us
    pallas_call x1, Pallas kernels, apply_inverse(): pl.pallas_call(functools.partial(apply_kernel, scale), out_shape=jax.Shap...  1.89 us

profile of v4, /device:TPU:0, one launch (start us, length us, event | category | flops | bytes accessed | tf_op | source)
XLA Modules:
  0.0 90.5 jit_solution(10709404820328578559)
XLA Ops:
  0.6 75.7 %shard_map.70.sketch = f32[1280,256]{1,0:T(8,128)S(1)} custom-call(s32[1,32]{1,0:T(1,128)} %bitcast.7, s32[1,32]{1,0:T(1,128)} %bitcast.8, s32[16,32]{1,0:T(8,128)} %bitcast.6, bf16[32,16,128,128]{3,2,1,0:T(8,128)(2,1)} %a_hbm.1, bf16[32,128,256]{2,1,0:T(8,128)(2,1)} %bitcast.5), custom_call_target="tpu_custom_call" | custom-call | tf_op jit(solution)/shard_map/pallas_call | solution.py:377
  76.4 11.2 %shard_map.71 = (f32[256,256]{1,0:T(8,128)S(1)}, f32[256,256]{1,0:T(8,128)}, f32[256,256]{1,0:T(8,128)S(1)}, s32[1]{0:T(128)}) custom-call(f32[1280,256]{1,0:T(8,128)S(1)} %shard_map.70.sketch), custom_call_target="tpu_custom_call" | custom-call | tf_op jit(solution)/shard_map/pallas_call | solution.py:514
  88.2 2.1 %conditional.1 = (f32[256,256]{1,0:T(8,128)}, f32[1024,256]{1,0:T(8,128)}) conditional(s32[]{:T(128)} %bitcast.4, (f32[256,256]{1,0:T(8,128)S(1)}, f32[1280,256]{1,0:T(8,128)S(1)}, f32[256,256]{1,0:T(8,128)}) %tuple.14, (f32[256,256]{1,0:T(8,128)S(1)}, f32[1280,256]{1,0:T(8,128)S(1)}, f32[256,256]{1,0:T(8,128)S(1)}) %tuple.15), branch_computations={%region_0.0_spmd, %region_1.0_spmd} | conditional | bytes 16 | solution.py:617
  88.2 1.9 %branch_0_fun.1 = f32[1024,256]{1,0:T(8,128)} custom-call(f32[256,256]{1,0:T(8,128)S(1)} %get-tuple-element.12.inverse, f32[1280,256]{1,0:T(8,128)S(1)} %get-tuple-element.13.sketch), custom_call_target="tpu_custom_call" | custom-call | tf_op jit(solution)/shard_map/cond/branch_0_fun/pallas_call | solution.py:541

commit v5 on v4

--- a/solution.py
+++ b/solution.py
@@ -15,7 +15,6 @@
 INFLATION = 2.0
 CHUNKS = 8
 WINDOW = 2
-TERMS = 4
 MESH = pl.DeviceIdType.MESH
 VMEM = pl.BlockSpec(memory_space=pltpu.VMEM)
 SMEM = pl.BlockSpec(memory_space=pltpu.SMEM)
@@ -256,6 +255,17 @@
     to_table.start()
     to_table.wait()
 
+    from_first = [(q, d) for q in range(chunks) for d in range(nc - 1, 0, -1)]
+    from_last = [(q, d) for q in range(chunks) for d in range(nc - 1)]
+
+    def start_ends(q, sends, buffer, hop):
+        for n, (at, d) in enumerate(sends):
+            if at == q:
+                if n >= WINDOW:
+                    hop(*sends[n - WINDOW]).wait_send()
+                buffer[q, d] = term[q % nc, d * RB_DEV:(d + 1) * RB_DEV].astype(jnp.bfloat16)
+                hop(q, d).start()
+
     def collect(q):
         keep_own(q).wait()
         for k in range(1, nr):
@@ -276,47 +286,35 @@
 
         @pl.loop(0, blocks, unroll=8)
         def _(b):
-            term[q % TERMS, b] = prefix[table[2, b]] * table[3, b].astype(jnp.float32)
+            term[q % nc, b] = prefix[table[2, b]] * table[3, b].astype(jnp.float32)
 
         @pl.when(c == 0)
         def _():
-            for d in range(nc - 1, 0, -1):
-                n = q * (nc - 1) + nc - 1 - d - WINDOW
-                if n >= 0:
-                    hop_right(n // (nc - 1), nc - 1 - n % (nc - 1)).wait_send()
-                to_right[q, d] = term[q % TERMS, d * RB_DEV:(d + 1) * RB_DEV].astype(jnp.bfloat16)
-                hop_right(q, d).start()
+            start_ends(q, from_first, to_right, hop_right)
 
         @pl.when(c == nc - 1)
         def _():
-            for d in range(nc - 1):
-                n = q * (nc - 1) + d - WINDOW
-                if n >= 0:
-                    hop_left(n // (nc - 1), n % (nc - 1)).wait_send()
-                to_left[q, d] = term[q % TERMS, d * RB_DEV:(d + 1) * RB_DEV].astype(jnp.bfloat16)
-                hop_left(q, d).start()
-
-    def pass_on(q):
-        for k in range(nc - 1, 0, -1):
-            @pl.when(jnp.logical_and(c > 0, c + k < nc))
-            def _():
-                d = c + k
-                hop_right(q, d).wait_recv()
-                mine = term[q % TERMS, pl.ds(d * RB_DEV, RB_DEV)]
-                to_right[q, d] = (to_right[q, d].astype(jnp.float32) + mine).astype(jnp.bfloat16)
-                hop_right(q, d).start()
-
-            @pl.when(jnp.logical_and(c < nc - 1, c - k >= 0))
-            def _():
-                d = c - k
-                hop_left(q, d).wait_recv()
-                mine = term[q % TERMS, pl.ds(d * RB_DEV, RB_DEV)]
-                to_left[q, d] = (to_left[q, d].astype(jnp.float32) + mine).astype(jnp.bfloat16)
-                hop_left(q, d).start()
-
+            start_ends(q, from_last, to_left, hop_left)
+
+    def add_and_send(q, d, buffer, hop):
+        hop(q, d).wait_recv()
+        mine = term[q % nc, d * RB_DEV:(d + 1) * RB_DEV]
+        buffer[q, d] = (buffer[q, d].astype(jnp.float32) + mine).astype(jnp.bfloat16)
+        hop(q, d).start()
+
+    def pass_on(q, hops):
+        @pl.when(c == hops)
+        def _():
+            for d in range(nc - 1, hops, -1):
+                add_and_send(q, d, to_right, hop_right)
+
+        @pl.when(c == nc - 1 - hops)
+        def _():
+            for d in range(nc - 1 - hops):
+                add_and_send(q, d, to_left, hop_left)
 
     def finish(q):
-        total[...] = term[q % TERMS, pl.ds(c * RB_DEV, RB_DEV)]
+        total[...] = term[q % nc, pl.ds(c * RB_DEV, RB_DEV)]
 
         @pl.when(c > 0)
         def _():
@@ -334,36 +332,37 @@
         rows = total[...].reshape(RB_DEV * rq, width)
         gram[...] += dot_tn(rows, rows)
 
-    for q in range(chunks + 2):
+    for q in range(chunks + nc - 1):
         if q < chunks:
             collect(q)
-        if 1 <= q <= chunks:
-            pass_on(q - 1)
-        if q >= 2:
-            finish(q - 2)
+        for hops in range(1, nc - 1):
+            if 0 <= q - hops < chunks:
+                pass_on(q - hops, hops)
+        if q >= nc - 1:
+            finish(q - nc + 1)
+
     sum_gram(nr, nc, r, c, gram, sketch_ref.at[pl.ds(RB_DEV * order, width)], *refs)
     for k in range(1, nr):
         route(k).wait_send()
+    for q in range(chunks):
+        for d in range(nc):
+            @pl.when(jnp.logical_and(c > 0, c < d))
+            def _():
+                hop_right(q, d).wait_send()
+
+            @pl.when(jnp.logical_and(c < nc - 1, c > d))
+            def _():
+                hop_left(q, d).wait_send()
 
     @pl.when(c == 0)
     def _():
-        for n in range(chunks * (nc - 1) - WINDOW, chunks * (nc - 1)):
-            hop_right(n // (nc - 1), nc - 1 - n % (nc - 1)).wait_send()
+        for send in from_first[-WINDOW:]:
+            hop_right(*send).wait_send()
 
     @pl.when(c == nc - 1)
     def _():
-        for n in range(chunks * (nc - 1) - WINDOW, chunks * (nc - 1)):
-            hop_left(n // (nc - 1), n % (nc - 1)).wait_send()
-
-    for q in range(chunks):
-        for k in range(1, nc):
-            @pl.when(jnp.logical_and(c > 0, c + k < nc))
-            def _():
-                hop_right(q, c + k).wait_send()
-
-            @pl.when(jnp.logical_and(c < nc - 1, c - k >= 0))
-            def _():
-                hop_left(q, c - k).wait_send()
+        for send in from_last[-WINDOW:]:
+            hop_left(*send).wait_send()
 
 
 def make_sketch(dest, target, col_target, a_blocks, omega, nr, nc):
@@ -394,7 +393,7 @@
             pltpu.VMEM((8, 128), jnp.int32),
             pltpu.SMEM((8, 128), jnp.int32),
             pltpu.VMEM((slots, rq, width), jnp.float32),
-            pltpu.VMEM((TERMS, blocks, rq, width), jnp.float32),
+            pltpu.VMEM((nc, blocks, rq, width), jnp.float32),
             hops, hops,
             pltpu.VMEM((RB_DEV, rq, width), jnp.float32),
             pltpu.VMEM((width, width), jnp.float32),
@@ -433,26 +432,29 @@
         j = 8 * g
         cols = [[jnp.broadcast_to(groups[i][:, j + l:j + l + 1], shape) for l in range(8)]
                 for i in range(g, rows // 8)]
-        piv = [[jnp.broadcast_to(cols[0][l][k:k + 1, :], shape) for l in range(8)] for k in range(8)]
+        piv = [[jnp.broadcast_to(cols[0][l][k:k + 1, :], shape) if l >= k else None for l in range(8)] for k in range(8)]
         tops = [jnp.broadcast_to(groups[g][k:k + 1, :], shape) for k in range(8)]
-        recip = []
+        ratio, scaled = [], []
         for k in range(8):
             if k % 2 == 0:
-                det = piv[k][k] * piv[k + 1][k + 1] - piv[k + 1][k] * piv[k][k + 1]
-                recip += [1.0 / piv[k][k], piv[k][k] * (1.0 / det)]
+                side = piv[k][k + 1]
+                det = piv[k][k] * piv[k + 1][k + 1] - side * side
+                recip, second = 1.0 / piv[k][k], piv[k][k] * (1.0 / det)
+            else:
+                recip = second
+            ratio.append([piv[k][l] * recip if l > k else None for l in range(8)])
+            scaled.append(tops[k] * recip)
             for m in range(k + 1, 8):
-                q = piv[m][k] * recip[k]
-                for l in range(k + 1, 8):
-                    piv[m][l] = piv[m][l] - q * piv[k][l]
-                tops[m] = tops[m] - q * tops[k]
+                for l in range(m, 8):
+                    piv[m][l] = piv[m][l] - ratio[k][m] * piv[k][l]
+                tops[m] = tops[m] - ratio[k][m] * tops[k]
         for i in range(g + 1, rows // 8):
             here = cols[i - g]
             value = groups[i]
             for k in range(8):
-                f = here[k] * recip[k]
                 for l in range(k + 1, 8):
-                    here[l] = here[l] - f * piv[k][l]
-                value = value - f * tops[k]
+                    here[l] = here[l] - here[k] * ratio[k][l]
+                value = value - here[k] * scaled[k]
             groups[i] = value
         for k in range(1, 8):
             groups[g] = jnp.where(sub == k, tops[k], groups[g])

time: 90.7 us -> 88.8 us (0.979)
  Pallas kernels: 88.8 us -> 87 us
    pallas_call x1, Pallas kernels: 75.7 us -> 74 us  [make_sketch(): pl.pallas_call(functools.partial(sketch_kernel, nr, nc), out_shape=jax.Sh...]
where the time goes in v5:
time: 88.8 us; the launch traced here: 88.7 us
  Pallas kernels  87 us (98%)
  between operations  1.48 us (2%)
    pallas_call x1, Pallas kernels, make_sketch(): pl.pallas_call(functools.partial(sketch_kernel, nr, nc), out_shape=jax.Sh...  74 us
    pallas_call x1, Pallas kernels, factor_first(): pl.pallas_call(functools.partial(factor_kernel, scale), out_shape=(square...  11.1 us
    pallas_call x1, Pallas kernels, apply_inverse(): pl.pallas_call(functools.partial(apply_kernel, scale), out_shape=jax.Shap...  1.89 us

profile of v5, /device:TPU:0, one launch (start us, length us, event | category | flops | bytes accessed | tf_op | source)
XLA Modules:
  0.0 88.7 jit_solution(1480890741049509448)
XLA Ops:
  0.6 74.0 %shard_map.70.sketch = f32[1280,256]{1,0:T(8,128)S(1)} custom-call(s32[1,32]{1,0:T(1,128)} %bitcast.7, s32[1,32]{1,0:T(1,128)} %bitcast.8, s32[16,32]{1,0:T(8,128)} %bitcast.6, bf16[32,16,128,128]{3,2,1,0:T(8,128)(2,1)} %a_hbm.1, bf16[32,128,256]{2,1,0:T(8,128)(2,1)} %bitcast.5), custom_call_target="tpu_custom_call" | custom-call | tf_op jit(solution)/shard_map/pallas_call | solution.py:376
  74.7 11.1 %shard_map.71 = (f32[256,256]{1,0:T(8,128)S(1)}, f32[256,256]{1,0:T(8,128)}, f32[256,256]{1,0:T(8,128)S(1)}, s32[1]{0:T(128)}) custom-call(f32[1280,256]{1,0:T(8,128)S(1)} %shard_map.70.sketch), custom_call_target="tpu_custom_call" | custom-call | tf_op jit(solution)/shard_map/pallas_call | solution.py:516
  86.4 2.1 %conditional.1 = (f32[256,256]{1,0:T(8,128)}, f32[1024,256]{1,0:T(8,128)}) conditional(s32[]{:T(128)} %bitcast.4, (f32[256,256]{1,0:T(8,128)S(1)}, f32[1280,256]{1,0:T(8,128)S(1)}, f32[256,256]{1,0:T(8,128)}) %tuple.14, (f32[256,256]{1,0:T(8,128)S(1)}, f32[1280,256]{1,0:T(8,128)S(1)}, f32[256,256]{1,0:T(8,128)S(1)}) %tuple.15), branch_computations={%region_0.0_spmd, %region_1.0_spmd} | conditional | bytes 16 | solution.py:619
  86.4 1.9 %branch_0_fun.1 = f32[1024,256]{1,0:T(8,128)} custom-call(f32[256,256]{1,0:T(8,128)S(1)} %get-tuple-element.12.inverse, f32[1280,256]{1,0:T(8,128)S(1)} %get-tuple-element.13.sketch), custom_call_target="tpu_custom_call" | custom-call | tf_op jit(solution)/shard_map/cond/branch_0_fun/pallas_call | solution.py:543

commit v6 on v5

--- a/solution.py
+++ b/solution.py
@@ -11,6 +11,7 @@
 CAP = 4
 PANEL = 64
 LOADS = 8
+FIRST = 4
 NOWHERE = 1 << 20
 INFLATION = 2.0
 CHUNKS = 8
@@ -67,41 +68,33 @@
     wait_all(nr, nc)
 
 
-def reduce_packed(nr, nc, r, c, gram, landed, cols, full, sems):
+def reduce_packed(nr, nc, r, c, packed, landed, cols, full, sems):
     a_s, a_r, b_s, b_r, c_s, c_r = sems
-    chunk = gram.shape[0] // nr
-    mine = pl.ds(pl.multiple_of(r * chunk, chunk), chunk)
-    copies = []
+    copies, across, back = [], [], []
     for k in range(1, nr):
         d = lax.rem(r + k, nr)
-        cp = pltpu.make_async_remote_copy(
-            gram.at[pl.ds(pl.multiple_of(d * chunk, chunk), chunk), :], landed.at[k], a_s.at[k], a_r.at[k],
-            device_id=(d, c), device_id_type=MESH)
-        cp.start()
-        copies.append(cp)
-    total = gram[mine, :]
+        copies.append(pltpu.make_async_remote_copy(
+            packed.at[d], landed.at[k], a_s.at[k], a_r.at[k], device_id=(d, c), device_id_type=MESH))
+        copies[-1].start()
+    total = packed[r]
     for k in range(1, nr):
         copies[k - 1].wait_recv()
         total = total + landed[k]
     cols[c] = total
-    across = []
     for k in range(1, nc):
-        cp = pltpu.make_async_remote_copy(
-            cols.at[c], cols.at[c], b_s.at[k], b_r.at[k], device_id=(r, lax.rem(c + k, nc)), device_id_type=MESH)
-        cp.start()
-        across.append(cp)
+        across.append(pltpu.make_async_remote_copy(
+            cols.at[c], cols.at[c], b_s.at[k], b_r.at[k], device_id=(r, lax.rem(c + k, nc)), device_id_type=MESH))
+        across[-1].start()
     for cp in across:
         cp.wait_recv()
     total = cols[0]
     for k in range(1, nc):
         total = total + cols[k]
-    full[mine, :] = total
-    back = []
+    full[r] = total
     for k in range(1, nr):
-        cp = pltpu.make_async_remote_copy(
-            full.at[mine, :], full.at[mine, :], c_s.at[k], c_r.at[k], device_id=(lax.rem(r + k, nr), c), device_id_type=MESH)
-        cp.start()
-        back.append(cp)
+        back.append(pltpu.make_async_remote_copy(
+            full.at[r], full.at[r], c_s.at[k], c_r.at[k], device_id=(lax.rem(r + k, nr), c), device_id_type=MESH))
+        back[-1].start()
     for cp in back:
         cp.wait_recv()
     for cp in copies + across + back:
@@ -110,29 +103,35 @@
 
 def packed_scratch(nr, nc, width):
     dma = pltpu.SemaphoreType.DMA
-    half = width // 2
-    chunk = 3 * half // nr
+    piece = (width // nr + 8, width // 2)
     return [
-        pltpu.VMEM((3 * half, half), jnp.float32),
-        pltpu.VMEM((nr, chunk, half), jnp.float32),
-        pltpu.VMEM((nc, chunk, half), jnp.float32),
-        pltpu.VMEM((3 * half, half), jnp.float32),
+        pltpu.VMEM((nr,) + piece, jnp.float32),
+        pltpu.VMEM((nr,) + piece, jnp.float32),
+        pltpu.VMEM((nc,) + piece, jnp.float32),
+        pltpu.VMEM((nr,) + piece, jnp.float32),
         dma((nr,)), dma((nr,)), dma((nc,)), dma((nc,)), dma((nr,)), dma((nr,)),
     ]
 
 
 def sum_gram(nr, nc, r, c, gram, out_ref, packed, landed, cols, full, *sems):
     half = gram.shape[0] // 2
-    packed[:half, :] = gram[:half, :half]
-    packed[half:2 * half, :] = gram[:half, half:]
-    packed[2 * half:, :] = gram[half:, half:]
+    main = 2 * half // nr
+    row = lax.broadcasted_iota(jnp.int32, (half, half), 0)
+    col = lax.broadcasted_iota(jnp.int32, (half, half), 1)
+    low = gram[half:, half:]
+    mixed = jnp.where(row <= col, gram[:half, :half], pltpu.roll(low, 1, 0))
+    for k in range(nr):
+        source, start = (gram[:half, half:], k * main) if k < nr // 2 else (mixed, k * main - half)
+        packed[k, :main] = source[start:start + main]
+        packed[k, main:] = jnp.broadcast_to(low[half - 1:half, :], (8, half))
     reduce_packed(nr, nc, r, c, packed, landed, cols, full, sems)
-    whole = full[...]
-    out_ref[:half, :half] = whole[:half]
-    side = whole[half:2 * half]
+    side = full[:nr // 2, :main].reshape(half, half)
+    mixed = full[nr // 2:, :main].reshape(half, half)
+    low = jnp.where(row == half - 1, jnp.broadcast_to(full[0, main:main + 1], (half, half)), pltpu.roll(mixed, half - 1, 0))
+    out_ref[:half, :half] = jnp.where(row <= col, mixed, mixed.T)
     out_ref[:half, half:] = side
     out_ref[half:, :half] = side.T
-    out_ref[half:, half:] = whole[2 * half:]
+    out_ref[half:, half:] = jnp.where(row >= col, low, low.T)
 
 
 def arrange(rows, slots):
@@ -165,13 +164,14 @@
     rq, width = order // chunks, omega_buf.shape[2]
     slots = nr * CAP
     blocks = nc * RB_DEV
-    loads = targets // LOADS
+    early = LOADS // FIRST
+    loads = targets // LOADS - 1
     r = lax.axis_index("row")
     c = lax.axis_index("col")
 
-    def fetch(i):
-        part = pl.ds(i * LOADS, LOADS)
-        return pltpu.make_async_copy(a_hbm.at[part], a_buf.at[part], a_sem.at[i])
+    def fetch(i, size, skip):
+        part = pl.ds(skip + i * size, size)
+        return pltpu.make_async_copy(a_hbm.at[part], a_buf.at[part], a_sem.at[skip // FIRST + i])
 
     def route(k):
         d = lax.rem(r + k, nr)
@@ -201,9 +201,31 @@
         ((dest_hbm, dest_ref), (target_hbm, target_ref), (col_hbm, col_ref), (omega_hbm, omega_buf)))]
     for copy in others:
         copy.start()
+    for i in range(early):
+        fetch(i, FIRST, 0).start()
     for i in range(loads):
-        fetch(i).start()
+        fetch(i, LOADS, LOADS).start()
     signal_all(nr, nc, r, c)
+    gram[...] = jnp.zeros_like(gram)
+    others[2].wait()
+    others[3].wait()
+
+    def multiply(i, carry, size, skip):
+        fetch(i, size, skip).wait()
+        for local in range(size):
+            t = skip + i * size + local
+            sums = None
+            for g in range(0, groups, 2):
+                left = jnp.concatenate([a_buf[t, g], a_buf[t, g + 1]], axis=1)
+                right = jnp.concatenate([omega_buf[col_ref[g, t]], omega_buf[col_ref[g + 1, t]]], axis=0)
+                product = jnp.dot(left, right, preferred_element_type=jnp.float32)
+                sums = product if sums is None else sums + product
+            sums = sums.astype(jnp.bfloat16)
+            for q in range(chunks):
+                parts[q, t] = sums[q * rq:(q + 1) * rq]
+        return carry
+
+    lax.fori_loop(0, early, functools.partial(multiply, size=FIRST, skip=0), 0)
     others[0].wait()
     others[1].wait()
     source, rows = place(dest_ref[...], target_ref[...], nr)
@@ -214,30 +236,10 @@
     to_sources.start()
     own_rows = pltpu.make_async_copy(row_ref.at[r], rows_in.at[r], own_s.at[chunks])
     own_rows.start()
-    gram[...] = jnp.zeros_like(gram)
-    others[2].wait()
-    others[3].wait()
-
-    def multiply(i, carry):
-        fetch(i).wait()
-        for local in range(LOADS):
-            t = i * LOADS + local
-            sums = None
-            for g in range(0, groups, 2):
-                left = jnp.concatenate([a_buf[t, g], a_buf[t, g + 1]], axis=1)
-                right = jnp.concatenate([omega_buf[col_ref[g, t]], omega_buf[col_ref[g + 1, t]]], axis=0)
-                product = jnp.dot(left, right, preferred_element_type=jnp.float32)
-                sums = product if sums is None else sums + product
-            sums = sums.astype(jnp.bfloat16)
-            for q in range(chunks):
-                parts[q, t] = sums[q * rq:(q + 1) * rq]
-        return carry
-
-    lax.fori_loop(0, loads // 2, multiply, 0)
     wait_all(nr, nc)
     for k in range(1, nr):
         route(k).start()
-    lax.fori_loop(loads // 2, loads, multiply, 0)
+    lax.fori_loop(0, loads, functools.partial(multiply, size=LOADS, skip=LOADS), 0)
     own_rows.wait()
     to_sources.wait()
     for q in range(chunks):
@@ -255,14 +257,23 @@
     to_table.start()
     to_table.wait()
 
-    from_first = [(q, d) for q in range(chunks) for d in range(nc - 1, 0, -1)]
-    from_last = [(q, d) for q in range(chunks) for d in range(nc - 1)]
-
-    def start_ends(q, sends, buffer, hop):
-        for n, (at, d) in enumerate(sends):
-            if at == q:
+    def in_turn(far, near):
+        turns = []
+        for q in range(chunks):
+            one = [(q, q, d) for d in far]
+            if q > 0:
+                one.insert(1, (q, q - 1, near))
+            turns += one
+        return turns + [(chunks - 1, chunks - 1, near)]
+
+    from_first = in_turn(list(range(nc - 1, 1, -1)), 1)
+    from_last = in_turn(list(range(nc - 2)), nc - 2)
+
+    def start_ends(now, sends, buffer, hop):
+        for n, (at, q, d) in enumerate(sends):
+            if at == now:
                 if n >= WINDOW:
-                    hop(*sends[n - WINDOW]).wait_send()
+                    hop(*sends[n - WINDOW][1:]).wait_send()
                 buffer[q, d] = term[q % nc, d * RB_DEV:(d + 1) * RB_DEV].astype(jnp.bfloat16)
                 hop(q, d).start()
 
@@ -335,7 +346,7 @@
     for q in range(chunks + nc - 1):
         if q < chunks:
             collect(q)
-        for hops in range(1, nc - 1):
+        for hops in range(nc - 2, 0, -1):
             if 0 <= q - hops < chunks:
                 pass_on(q - hops, hops)
         if q >= nc - 1:
@@ -357,12 +368,12 @@
     @pl.when(c == 0)
     def _():
         for send in from_first[-WINDOW:]:
-            hop_right(*send).wait_send()
+            hop_right(*send[1:]).wait_send()
 
     @pl.when(c == nc - 1)
     def _():
         for send in from_last[-WINDOW:]:
-            hop_left(*send).wait_send()
+            hop_left(*send[1:]).wait_send()
 
 
 def make_sketch(dest, target, col_target, a_blocks, omega, nr, nc):
@@ -388,7 +399,7 @@
             pltpu.VMEM((chunks, nr, CAP, rq, width), jnp.bfloat16),
             pltpu.VMEM((nr, 8, 128), jnp.int32),
             pltpu.SMEM((8, 128), jnp.int32),
-            dma((targets // LOADS,)), dma((4,)),
+            dma((targets // FIRST,)), dma((4,)),
             pltpu.VMEM((nr, 8, 128), jnp.int32),
             pltpu.VMEM((8, 128), jnp.int32),
             pltpu.SMEM((8, 128), jnp.int32),
@@ -434,27 +445,25 @@
                 for i in range(g, rows // 8)]
         piv = [[jnp.broadcast_to(cols[0][l][k:k + 1, :], shape) if l >= k else None for l in range(8)] for k in range(8)]
         tops = [jnp.broadcast_to(groups[g][k:k + 1, :], shape) for k in range(8)]
-        ratio, scaled = [], []
+        recip = []
         for k in range(8):
             if k % 2 == 0:
                 side = piv[k][k + 1]
                 det = piv[k][k] * piv[k + 1][k + 1] - side * side
-                recip, second = 1.0 / piv[k][k], piv[k][k] * (1.0 / det)
-            else:
-                recip = second
-            ratio.append([piv[k][l] * recip if l > k else None for l in range(8)])
-            scaled.append(tops[k] * recip)
+                recip += [1.0 / piv[k][k], piv[k][k] * (1.0 / det)]
             for m in range(k + 1, 8):
+                q = piv[k][m] * recip[k]
                 for l in range(m, 8):
-                    piv[m][l] = piv[m][l] - ratio[k][m] * piv[k][l]
-                tops[m] = tops[m] - ratio[k][m] * tops[k]
+                    piv[m][l] = piv[m][l] - q * piv[k][l]
+                tops[m] = tops[m] - q * tops[k]
         for i in range(g + 1, rows // 8):
             here = cols[i - g]
             value = groups[i]
             for k in range(8):
+                f = here[k] * recip[k]
                 for l in range(k + 1, 8):
-                    here[l] = here[l] - here[k] * ratio[k][l]
-                value = value - here[k] * scaled[k]
+                    here[l] = here[l] - f * piv[k][l]
+                value = value - f * tops[k]
             groups[i] = value
         for k in range(1, 8):
             groups[g] = jnp.where(sub == k, tops[k], groups[g])

time: 88.8 us -> 87.8 us (0.989)
  Pallas kernels: 87 us -> 85.9 us
where the time goes in v6:
time: 87.8 us; the launch traced here: 87.6 us
  Pallas kernels  85.9 us (98%)
  between operations  1.48 us (2%)
    pallas_call x1, Pallas kernels, make_sketch(): pl.pallas_call(functools.partial(sketch_kernel, nr, nc), out_shape=jax.Sh...  73.8 us
    pallas_call x1, Pallas kernels, factor_first(): pl.pallas_call(functools.partial(factor_kernel, scale), out_shape=(square...  10.2 us
    pallas_call x1, Pallas kernels, apply_inverse(): pl.pallas_call(functools.partial(apply_kernel, scale), out_shape=jax.Shap...  1.89 us

profile of v6, /device:TPU:0, one launch (start us, length us, event | category | flops | bytes accessed | tf_op | source)
XLA Modules:
  0.0 87.6 jit_solution(10519806276056857366)
XLA Ops:
  0.6 73.8 %shard_map.70.sketch = f32[1280,256]{1,0:T(8,128)S(1)} custom-call(s32[1,32]{1,0:T(1,128)} %bitcast.7, s32[1,32]{1,0:T(1,128)} %bitcast.8, s32[16,32]{1,0:T(8,128)} %bitcast.6, bf16[32,16,128,128]{3,2,1,0:T(8,128)(2,1)} %a_hbm.1, bf16[32,128,256]{2,1,0:T(8,128)(2,1)} %bitcast.5), custom_call_target="tpu_custom_call" | custom-call | tf_op jit(solution)/shard_map/pallas_call | solution.py:387
  74.5 10.2 %shard_map.71 = (f32[256,256]{1,0:T(8,128)S(1)}, f32[256,256]{1,0:T(8,128)}, f32[256,256]{1,0:T(8,128)S(1)}, s32[1]{0:T(128)}) custom-call(f32[1280,256]{1,0:T(8,128)S(1)} %shard_map.70.sketch), custom_call_target="tpu_custom_call" | custom-call | tf_op jit(solution)/shard_map/pallas_call | solution.py:525
  85.3 2.1 %conditional.1 = (f32[256,256]{1,0:T(8,128)}, f32[1024,256]{1,0:T(8,128)}) conditional(s32[]{:T(128)} %bitcast.4, (f32[256,256]{1,0:T(8,128)S(1)}, f32[1280,256]{1,0:T(8,128)S(1)}, f32[256,256]{1,0:T(8,128)}) %tuple.14, (f32[256,256]{1,0:T(8,128)S(1)}, f32[1280,256]{1,0:T(8,128)S(1)}, f32[256,256]{1,0:T(8,128)S(1)}) %tuple.15), branch_computations={%region_0.0_spmd, %region_1.0_spmd} | conditional | bytes 16 | solution.py:628
  85.3 1.9 %branch_0_fun.1 = f32[1024,256]{1,0:T(8,128)} custom-call(f32[256,256]{1,0:T(8,128)S(1)} %get-tuple-element.12.inverse, f32[1280,256]{1,0:T(8,128)S(1)} %get-tuple-element.13.sketch), custom_call_target="tpu_custom_call" | custom-call | tf_op jit(solution)/shard_map/cond/branch_0_fun/pallas_call | solution.py:552

commit v7 on v6

--- a/solution.py
+++ b/solution.py
@@ -346,10 +346,12 @@
     for q in range(chunks + nc - 1):
         if q < chunks:
             collect(q)
+        if q == chunks:
+            finish(q - nc + 1)
         for hops in range(nc - 2, 0, -1):
             if 0 <= q - hops < chunks:
                 pass_on(q - hops, hops)
-        if q >= nc - 1:
+        if q >= nc - 1 and q != chunks:
             finish(q - nc + 1)
 
     sum_gram(nr, nc, r, c, gram, sketch_ref.at[pl.ds(RB_DEV * order, width)], *refs)

time: 87.8 us -> 87.3 us (level)
  no operation moved by 1% of the time
where the time goes in v7:
time: 87.3 us; the launch traced here: 87.1 us
  Pallas kernels  85.4 us (98%)
  between operations  1.48 us (2%)
    pallas_call x1, Pallas kernels, make_sketch(): pl.pallas_call(functools.partial(sketch_kernel, nr, nc), out_shape=jax.Sh...  73.3 us
    pallas_call x1, Pallas kernels, factor_first(): pl.pallas_call(functools.partial(factor_kernel, scale), out_shape=(square...  10.2 us
    pallas_call x1, Pallas kernels, apply_inverse(): pl.pallas_call(functools.partial(apply_kernel, scale), out_shape=jax.Shap...  1.89 us

profile of v7, /device:TPU:0, one launch (start us, length us, event | category | flops | bytes accessed | tf_op | source)
XLA Modules:
  0.0 87.1 jit_solution(10924402912863119049)
XLA Ops:
  0.6 73.3 %shard_map.70.sketch = f32[1280,256]{1,0:T(8,128)S(1)} custom-call(s32[1,32]{1,0:T(1,128)} %bitcast.7, s32[1,32]{1,0:T(1,128)} %bitcast.8, s32[16,32]{1,0:T(8,128)} %bitcast.6, bf16[32,16,128,128]{3,2,1,0:T(8,128)(2,1)} %a_hbm.1, bf16[32,128,256]{2,1,0:T(8,128)(2,1)} %bitcast.5), custom_call_target="tpu_custom_call" | custom-call | tf_op jit(solution)/shard_map/pallas_call | solution.py:389
  74.0 10.2 %shard_map.71 = (f32[256,256]{1,0:T(8,128)S(1)}, f32[256,256]{1,0:T(8,128)}, f32[256,256]{1,0:T(8,128)S(1)}, s32[1]{0:T(128)}) custom-call(f32[1280,256]{1,0:T(8,128)S(1)} %shard_map.70.sketch), custom_call_target="tpu_custom_call" | custom-call | tf_op jit(solution)/shard_map/pallas_call | solution.py:527
  84.8 2.1 %conditional.1 = (f32[256,256]{1,0:T(8,128)}, f32[1024,256]{1,0:T(8,128)}) conditional(s32[]{:T(128)} %bitcast.4, (f32[256,256]{1,0:T(8,128)S(1)}, f32[1280,256]{1,0:T(8,128)S(1)}, f32[256,256]{1,0:T(8,128)}) %tuple.14, (f32[256,256]{1,0:T(8,128)S(1)}, f32[1280,256]{1,0:T(8,128)S(1)}, f32[256,256]{1,0:T(8,128)S(1)}) %tuple.15), branch_computations={%region_0.0_spmd, %region_1.0_spmd} | conditional | bytes 16 | solution.py:630
  84.8 1.9 %branch_0_fun.1 = f32[1024,256]{1,0:T(8,128)} custom-call(f32[256,256]{1,0:T(8,128)S(1)} %get-tuple-element.12.inverse, f32[1280,256]{1,0:T(8,128)S(1)} %get-tuple-element.13.sketch), custom_call_target="tpu_custom_call" | custom-call | tf_op jit(solution)/shard_map/cond/branch_0_fun/pallas_call | solution.py:554

commit v8 on v7

--- a/solution.py
+++ b/solution.py
@@ -293,9 +293,9 @@
             prefix[k] = acc
             return acc
 
-        lax.fori_loop(0, slots, add, jnp.zeros((rq, width), jnp.float32), unroll=8)
-
-        @pl.loop(0, blocks, unroll=8)
+        lax.fori_loop(0, slots, add, jnp.zeros((rq, width), jnp.float32), unroll=16)
+
+        @pl.loop(0, blocks, unroll=16)
         def _(b):
             term[q % nc, b] = prefix[table[2, b]] * table[3, b].astype(jnp.float32)
 

time: 87.3 us -> 87.2 us (level)
  no operation moved by 1% of the time
where the time goes in v8:
time: 87.2 us; the launch traced here: 87.1 us
  Pallas kernels  85.4 us (98%)
  between operations  1.48 us (2%)
    pallas_call x1, Pallas kernels, make_sketch(): pl.pallas_call(functools.partial(sketch_kernel, nr, nc), out_shape=jax.Sh...  73.3 us
    pallas_call x1, Pallas kernels, factor_first(): pl.pallas_call(functools.partial(factor_kernel, scale), out_shape=(square...  10.2 us
    pallas_call x1, Pallas kernels, apply_inverse(): pl.pallas_call(functools.partial(apply_kernel, scale), out_shape=jax.Shap...  1.89 us

profile of v8, /device:TPU:0, one launch (start us, length us, event | category | flops | bytes accessed | tf_op | source)
XLA Modules:
  0.0 87.1 jit_solution(10379775147388904140)
XLA Ops:
  0.6 73.3 %shard_map.70.sketch = f32[1280,256]{1,0:T(8,128)S(1)} custom-call(s32[1,32]{1,0:T(1,128)} %bitcast.7, s32[1,32]{1,0:T(1,128)} %bitcast.8, s32[16,32]{1,0:T(8,128)} %bitcast.6, bf16[32,16,128,128]{3,2,1,0:T(8,128)(2,1)} %a_hbm.1, bf16[32,128,256]{2,1,0:T(8,128)(2,1)} %bitcast.5), custom_call_target="tpu_custom_call" | custom-call | tf_op jit(solution)/shard_map/pallas_call | solution.py:389
  73.9 10.2 %shard_map.71 = (f32[256,256]{1,0:T(8,128)S(1)}, f32[256,256]{1,0:T(8,128)}, f32[256,256]{1,0:T(8,128)S(1)}, s32[1]{0:T(128)}) custom-call(f32[1280,256]{1,0:T(8,128)S(1)} %shard_map.70.sketch), custom_call_target="tpu_custom_call" | custom-call | tf_op jit(solution)/shard_map/pallas_call | solution.py:527
  84.8 2.1 %conditional.1 = (f32[256,256]{1,0:T(8,128)}, f32[1024,256]{1,0:T(8,128)}) conditional(s32[]{:T(128)} %bitcast.4, (f32[256,256]{1,0:T(8,128)S(1)}, f32[1280,256]{1,0:T(8,128)S(1)}, f32[256,256]{1,0:T(8,128)}) %tuple.14, (f32[256,256]{1,0:T(8,128)S(1)}, f32[1280,256]{1,0:T(8,128)S(1)}, f32[256,256]{1,0:T(8,128)S(1)}) %tuple.15), branch_computations={%region_0.0_spmd, %region_1.0_spmd} | conditional | bytes 16 | solution.py:630
  84.8 1.9 %branch_0_fun.1 = f32[1024,256]{1,0:T(8,128)} custom-call(f32[256,256]{1,0:T(8,128)S(1)} %get-tuple-element.12.inverse, f32[1280,256]{1,0:T(8,128)S(1)} %get-tuple-element.13.sketch), custom_call_target="tpu_custom_call" | custom-call | tf_op jit(solution)/shard_map/cond/branch_0_fun/pallas_call | solution.py:554
